TPU v7x, 1024 devices: a whole 4x4x32 slice. The times are simulated.
1024 devices in a mesh: replica: 128 (over z_hi, y, x, core), expert: 8 (over z_lo).
Axes of the slice: x: 4, y: 4, z: 32 (z_hi: 4, z_lo: 8; z = z_hi * 8 + z_lo), core: 2. Of those that a mesh axis runs over, the one named last changes fastest.
Arguments:
- tokens: bfloat16 [131072, 1024], P(('replica', 'expert')), may hold values from -6 to 6
- cotangent: bfloat16 [131072, 1024], P(('replica', 'expert')), may hold values from -6 to 6
- expert_ids: int32 [131072, 8], P(('replica', 'expert')), may hold values from 0 to 63, as said below
- gate_weights: float32 [131072, 8], P(('replica', 'expert')), may hold values from 0.05 to 0.5
- gate_up: bfloat16 [8, 1024, 1024], P('expert'), may hold values from -0.1875 to 0.1875
- down_weights: bfloat16 [128, 8, 512, 1024], P('replica', 'expert'), may hold values from -6 to 6
Outputs:
- layer_out: bfloat16 [131072, 1024], P(('replica', 'expert'))
- token_grad: bfloat16 [131072, 1024], P(('replica', 'expert'))
- mixed_down: bfloat16 [128, 8, 512, 1024], P('replica', 'expert')
Inputs may be any that keep to these rules, and one draw needn't show every extreme that they name: `expert_ids`: each token names 8 distinct experts. Among the 128 tokens of one device, each expert below 8 is named by at most 16 tokens; in every replica one such expert is named by exactly 16 tokens of each of its 8 devices.
All inputs are finite; a program needn't handle non-finite values.
Results may differ from a plain program's by a relative error of at most 0.0075.
Values may be sent and summed in bfloat16 or wider, within the bound.
No kernel may reach another device: no remote copies, remote signals or barrier semaphores. Data moves between devices by JAX's collectives and lax.ppermute only.
A program may use at most 32 MiB of HBM per device.

v0:
```python
import jax
import jax.numpy as jnp
from jax import lax
from jax.sharding import PartitionSpec as P

CAP = 16


step_size = 2.0
mix_share = 0.5


def passed_along(block, axis, distance):
    devices = range(lax.axis_size(axis))
    route = [((i - distance) % len(devices), i) for i in devices]
    return lax.ppermute(block, axis, route)


def silu_parts(pre):
    sigmoid_value = jax.nn.sigmoid(pre)
    return (pre * sigmoid_value, sigmoid_value * (1.0 + pre * (1.0 - sigmoid_value)))


def weight_step(weights, hidden, routed):
    weight_scale = weights.shape[0] ** (-0.5)
    weight_grad = (
        lax.dot_general(
            hidden, routed, (((0,), (0,)), ((), ())), preferred_element_type=jnp.float32
        )
        * weight_scale
    )
    return (weights.astype(jnp.float32) - step_size * weight_grad).astype(jnp.bfloat16)


def expert_pass(inputs, routed, project, weights):
    hidden_width = weights.shape[0]
    weight_scale = hidden_width ** (-0.5)
    projected = jnp.dot(inputs, project, preferred_element_type=jnp.float32)
    gate_pre = projected[:, :hidden_width]
    up_pre = projected[:, hidden_width:]
    activated, act_slope = silu_parts(gate_pre)
    hidden = (activated * up_pre).astype(jnp.bfloat16)
    outputs = (jnp.dot(hidden, weights, preferred_element_type=jnp.float32) * weight_scale).astype(
        jnp.bfloat16
    )
    hidden_grad = (
        lax.dot_general(
            routed, weights, (((1,), (1,)), ((), ())), preferred_element_type=jnp.float32
        )
        * weight_scale
    )
    pre_grad = jnp.concatenate(
        [hidden_grad * up_pre * act_slope, hidden_grad * activated], axis=1
    ).astype(jnp.bfloat16)
    input_grad = lax.dot_general(
        pre_grad, project, (((1,), (1,)), ((), ())), preferred_element_type=jnp.float32
    ).astype(jnp.bfloat16)
    return (outputs, input_grad, hidden)


def on_device(tokens, cotangent, expert_ids, gate_weights, gate_up, down_weights):
    experts = lax.axis_size("expert")
    capacity = CAP
    model_width = tokens.shape[1]
    weights = down_weights[0, 0]
    project = gate_up[0]
    expert_lane = jnp.arange(experts, dtype=jnp.int32)
    slot_hits = expert_ids[:, :, None] == expert_lane[None, None, :]
    expert_named = jnp.any(slot_hits, axis=1).astype(jnp.int32)
    gate_share = jnp.sum(jnp.where(slot_hits, gate_weights[:, :, None], 0.0), axis=1)
    position = jnp.cumsum(expert_named, axis=0) - 1
    slot_lane = jnp.arange(capacity, dtype=jnp.int32)
    picked = (expert_named.T[:, None, :] == 1) & (
        position.T[:, None, :] == slot_lane[None, :, None]
    )
    picked_bf16 = picked.astype(jnp.bfloat16)
    slot_share = jnp.sum(picked.astype(jnp.float32) * gate_share.T[:, None, :], axis=2)
    inputs = jnp.einsum(
        "ect,td->ecd", picked_bf16, tokens, preferred_element_type=jnp.float32
    ).astype(jnp.bfloat16)
    picked_cot = jnp.einsum(
        "ect,td->ecd", picked_bf16, cotangent, preferred_element_type=jnp.float32
    )
    routed = (slot_share[:, :, None] * picked_cot).astype(jnp.bfloat16)
    arrived = (
        lax.all_to_all(inputs, "expert", split_axis=0, concat_axis=0, tiled=True),
        lax.all_to_all(routed, "expert", split_axis=0, concat_axis=0, tiled=True),
    )
    arrived_inputs = arrived[0].reshape(experts * capacity, model_width)
    arrived_routed = arrived[1].reshape(experts * capacity, model_width)
    outputs, input_grad, hidden = expert_pass(arrived_inputs, arrived_routed, project, weights)
    came_back = (
        lax.all_to_all(
            outputs.reshape(experts, capacity, model_width),
            "expert",
            split_axis=0,
            concat_axis=0,
            tiled=True,
        ),
        lax.all_to_all(
            input_grad.reshape(experts, capacity, model_width),
            "expert",
            split_axis=0,
            concat_axis=0,
            tiled=True,
        ),
    )
    scaled_out = slot_share[:, :, None] * came_back[0].astype(jnp.float32)
    upper_part = scaled_out.astype(jnp.bfloat16)
    lower_part = (scaled_out - upper_part.astype(jnp.float32)).astype(jnp.bfloat16)
    layer_sum = jnp.einsum(
        "ect,ecd->td", picked_bf16, upper_part, preferred_element_type=jnp.float32
    )
    layer_sum = layer_sum + jnp.einsum(
        "ect,ecd->td", picked_bf16, lower_part, preferred_element_type=jnp.float32
    )
    layer_out = layer_sum.astype(jnp.bfloat16)
    token_grad = jnp.einsum(
        "ect,ecd->td", picked_bf16, came_back[1], preferred_element_type=jnp.float32
    ).astype(jnp.bfloat16)
    updated = weight_step(weights, hidden, arrived_routed)
    neighbor = passed_along(updated, "replica", 1)
    mixed_down = (
        (1.0 - mix_share) * updated.astype(jnp.float32) + mix_share * neighbor.astype(jnp.float32)
    ).astype(jnp.bfloat16)
    return (layer_out, token_grad, mixed_down[None, None])


def solution(mesh):
    return jax.shard_map(
        on_device,
        mesh=mesh,
        in_specs=(
            P(("replica", "expert"), None),
            P(("replica", "expert"), None),
            P(("replica", "expert"), None),
            P(("replica", "expert"), None),
            P("expert", None, None),
            P("replica", "expert", None, None),
        ),
        out_specs=(
            P(("replica", "expert"), None),
            P(("replica", "expert"), None),
            P("replica", "expert", None, None),
        ),
        check_vma=False,
    )
```

profile of v0, /device:TPU:128, one launch (start us, length us, event | category | flops | bytes accessed | tf_op | source)
XLA Modules:
  0.0 204.5 jit_solution(9137272474107268198)
XLA Ops:
  0.6 0.0 copy-start
  0.6 0.8 fusion.36
  1.5 0.1 copy.13
  1.6 0.2 reduce_window_sum.11
  1.8 1.9 convolution_convert_fusion
  3.7 14.7 %all-to-all-start = ((bf16[8,16,1024]{2,1,0:T(8,128)(2,1)}), bf16[8,16,1024]{2,1,0:T(8,128)(2,1)S(1)}, u32[]{:S(2)}, u32[]{:S(2)}) async-start(bf16[8,16,1024]{2,1,0:T(8,128)(2,1)} %convolution_convert_fusion), calls=%async_computation | async-start | bytes 524288 | tf_op jit(solution)/shard_map/all_to_all | solution.py:86
  18.4 0.0 copy-start.1
  18.4 0.8 select_reduce_fusion.1
  19.2 0.1 select_reduce_fusion
  19.3 1.9 fusion.6
  21.2 5.6 %all-to-all-done = bf16[8,16,1024]{2,1,0:T(8,128)(2,1)S(1)} async-done(((bf16[8,16,1024]{2,1,0:T(8,128)(2,1)}), bf16[8,16,1024]{2,1,0:T(8,128)(2,1)S(1)}, u32[]{:S(2)}, u32[]{:S(2)}) %all-to-all-start) | async-done | bytes 262176 | tf_op jit(solution)/shard_map/all_to_all | solution.py:86
  26.8 0.0 copy-start.5
  26.8 0.7 copy-done.5
  27.5 9.9 %all-to-all-start.2 = ((bf16[8,16,1024]{2,1,0:T(8,128)(2,1)}), bf16[8,16,1024]{2,1,0:T(8,128)(2,1)S(1)}, u32[]{:S(2)}, u32[]{:S(2)}) async-start(bf16[8,16,1024]{2,1,0:T(8,128)(2,1)} %fusion.6), calls=%async_computation.2 | async-start | bytes 524288 | tf_op jit(solution)/shard_map/all_to_all | solution.py:87
  37.4 0.0 copy-done
  37.4 2.2 %fusion.2 = f32[128,1024]{1,0:T(8,128)} fusion(bf16[128,1024]{1,0:T(8,128)(2,1)} %bitcast.54, bf16[1,1024,1024]{2,1,0:T(8,128)(2,1)S(1)} %copy-done), kind=kOutput, calls=%fused_computation.2 | convolution fusion | flops 268435456 | bytes 2883584 | tf_op jit(solution)/shard_map/dot_general | solution.py:38
  39.6 8.2 %all-to-all-done.2 = bf16[8,16,1024]{2,1,0:T(8,128)(2,1)S(1)} async-done(((bf16[8,16,1024]{2,1,0:T(8,128)(2,1)}), bf16[8,16,1024]{2,1,0:T(8,128)(2,1)S(1)}, u32[]{:S(2)}, u32[]{:S(2)}) %all-to-all-start.2) | async-done | bytes 262176 | tf_op jit(solution)/shard_map/all_to_all | solution.py:87
  47.8 0.0 copy-start.2
  47.8 0.0 copy-done.1
  47.8 1.7 multiply_convert_fusion.2
  49.5 1.6 fusion.9
  51.0 0.0 copy-done.2
  51.0 10.3 %all-to-all-start.3 = ((bf16[8,16,1024]{2,1,0:T(8,128)(2,1)}), bf16[8,16,1024]{2,1,0:T(8,128)(2,1)S(1)}, u32[]{:S(2)}, u32[]{:S(2)}) async-start(bf16[8,16,1024]{2,1,0:T(8,128)(2,1)} %bitcast.52), calls=%async_computation.3 | async-start | bytes 524288 | tf_op jit(solution)/shard_map/all_to_all | solution.py:100
  61.3 1.0 fusion.8
  62.3 10.1 %all-to-all-done.3 = bf16[8,16,1024]{2,1,0:T(8,128)(2,1)S(1)} async-done(((bf16[8,16,1024]{2,1,0:T(8,128)(2,1)}), bf16[8,16,1024]{2,1,0:T(8,128)(2,1)S(1)}, u32[]{:S(2)}, u32[]{:S(2)}) %all-to-all-start.3) | async-done | bytes 262176 | tf_op jit(solution)/shard_map/all_to_all | solution.py:100
  72.4 0.0 copy-start.3
  72.4 0.7 copy-done.3
  73.1 10.3 %all-to-all-start.1 = ((bf16[8,16,1024]{2,1,0:T(8,128)(2,1)}), bf16[8,16,1024]{2,1,0:T(8,128)(2,1)S(1)}, u32[]{:S(2)}, u32[]{:S(2)}) async-start(bf16[8,16,1024]{2,1,0:T(8,128)(2,1)} %bitcast.53), calls=%async_computation.1 | async-start | bytes 524288 | tf_op jit(solution)/shard_map/all_to_all | solution.py:93
  83.4 1.4 subtract_convert_fusion
  84.8 0.0 copy-start.4
  84.8 2.1 %collective-permute-start = (bf16[512,1024]{1,0:T(8,128)(2,1)S(1)}, bf16[512,1024]{1,0:T(8,128)(2,1)S(1)}, u32[]{:S(2)}, u32[]{:S(2)}) collective-permute-start(bf16[512,1024]{1,0:T(8,128)(2,1)S(1)} %subtract_convert_fusion), channel_id=1, source_target_pairs={{1016,0},{0,8},{8,16},{16,24},{24,32},{32,40},{40,48},{48,56},{56,... | collective-permute-start | bytes 3145736 | tf_op jit(solution)/shard_map/ppermute | solution.py:16
  86.9 113.9 %collective-permute-done = bf16[512,1024]{1,0:T(8,128)(2,1)S(1)} collective-permute-done((bf16[512,1024]{1,0:T(8,128)(2,1)S(1)}, bf16[512,1024]{1,0:T(8,128)(2,1)S(1)}, u32[]{:S(2)}, u32[]{:S(2)}) %collective-permute-start) | collective-permute-done | bytes 1048608 | tf_op jit(solution)/shard_map/ppermute | solution.py:16
  200.8 1.4 fusion.12
  202.2 0.0 copy-done.4
  202.2 1.0 fusion.7
  203.2 0.0 all-to-all-done.1
  203.2 0.3 convolution_bitcast_fusion.1
  203.5 1.0 fusion.5
  (3 shorter events, 0.1 us)
Async XLA Ops:
  0.6 36.8 %copy-start = (bf16[1,1024,1024]{2,1,0:T(8,128)(2,1)S(1)}, bf16[1,1024,1024]{2,1,0:T(8,128)(2,1)}, u32[]{:S(2)}) copy-start(bf16[1,1024,1024]{2,1,0:T(8,128)(2,1)} %param.10) | copy-start | bytes 6291460
  3.7 23.1 %all-to-all-start = ((bf16[8,16,1024]{2,1,0:T(8,128)(2,1)}), bf16[8,16,1024]{2,1,0:T(8,128)(2,1)S(1)}, u32[]{:S(2)}, u32[]{:S(2)}) async-start(bf16[8,16,1024]{2,1,0:T(8,128)(2,1)} %convolution_convert_fusion), calls=%async_computation | async-start | bytes 524288 | tf_op jit(solution)/shard_map/all_to_all | solution.py:86
  18.4 29.4 %copy-start.1 = (bf16[1,1,512,1024]{3,2,1,0:T(8,128)(2,1)S(1)}, bf16[1,1,512,1024]{3,2,1,0:T(8,128)(2,1)}, u32[]{:S(2)}) copy-start(bf16[1,1,512,1024]{3,2,1,0:T(8,128)(2,1)} %param.11) | copy-start | bytes 3145732
  26.8 0.7 copy-start.5
  27.5 20.3 %all-to-all-start.2 = ((bf16[8,16,1024]{2,1,0:T(8,128)(2,1)}), bf16[8,16,1024]{2,1,0:T(8,128)(2,1)S(1)}, u32[]{:S(2)}, u32[]{:S(2)}) async-start(bf16[8,16,1024]{2,1,0:T(8,128)(2,1)} %fusion.6), calls=%async_computation.2 | async-start | bytes 524288 | tf_op jit(solution)/shard_map/all_to_all | solution.py:87
  47.8 3.2 %copy-start.2 = (bf16[8,16,1024]{2,1,0:T(8,128)(2,1)}, bf16[8,16,1024]{2,1,0:T(8,128)(2,1)S(1)}, u32[]{:S(2)}) copy-start(bf16[8,16,1024]{2,1,0:T(8,128)(2,1)S(1)} %all-to-all-done.2) | copy-start | bytes 786436
  51.0 21.4 %all-to-all-start.3 = ((bf16[8,16,1024]{2,1,0:T(8,128)(2,1)}), bf16[8,16,1024]{2,1,0:T(8,128)(2,1)S(1)}, u32[]{:S(2)}, u32[]{:S(2)}) async-start(bf16[8,16,1024]{2,1,0:T(8,128)(2,1)} %bitcast.52), calls=%async_computation.3 | async-start | bytes 524288 | tf_op jit(solution)/shard_map/all_to_all | solution.py:100
  72.4 0.7 copy-start.3
  73.1 130.1 %all-to-all-start.1 = ((bf16[8,16,1024]{2,1,0:T(8,128)(2,1)}), bf16[8,16,1024]{2,1,0:T(8,128)(2,1)S(1)}, u32[]{:S(2)}, u32[]{:S(2)}) async-start(bf16[8,16,1024]{2,1,0:T(8,128)(2,1)} %bitcast.53), calls=%async_computation.1 | async-start | bytes 524288 | tf_op jit(solution)/shard_map/all_to_all | solution.py:93
  84.8 117.4 %copy-start.4 = (bf16[8,16,1024]{2,1,0:T(8,128)(2,1)S(1)}, bf16[8,16,1024]{2,1,0:T(8,128)(2,1)}, u32[]{:S(2)}) copy-start(bf16[8,16,1024]{2,1,0:T(8,128)(2,1)} %copy-done.3) | copy-start | bytes 786436
  84.8 116.0 %collective-permute-start = (bf16[512,1024]{1,0:T(8,128)(2,1)S(1)}, bf16[512,1024]{1,0:T(8,128)(2,1)S(1)}, u32[]{:S(2)}, u32[]{:S(2)}) collective-permute-start(bf16[512,1024]{1,0:T(8,128)(2,1)S(1)} %subtract_convert_fusion), channel_id=1, source_target_pairs={{1016,0},{0,8},{8,16},{16,24},{24,32},{32,40},{40,48},{48,56},{56,... | collective-permute-start | bytes 3145736 | tf_op jit(solution)/shard_map/ppermute | solution.py:16
where the time goes:
time: 205 us
  waiting for transfers between devices  138 us (67%)
  starting transfers between devices  47.2 us (23%)
  matrix products  13.9 us (7%)
  other arithmetic  3.32 us (2%)
    ppermute x1, waiting for transfers between devices, passed_along(): return lax.ppermute(block, axis, route)  114 us
    all_to_all x1, starting transfers between devices, on_device(): lax.all_to_all(inputs, 'expert', split_axis=0, concat_axis=0, tiled=True)  14.7 us
    all_to_all x1, starting transfers between devices, on_device(): lax.all_to_all(outputs.reshape(experts, capacity, model_width), 'expert',...  10.3 us
    all_to_all x1, starting transfers between devices, on_device(): lax.all_to_all(input_grad.reshape(experts, capacity, model_width), 'exper...  10.3 us
    all_to_all x1, waiting for transfers between devices, on_device(): lax.all_to_all(input_grad.reshape(experts, capacity, model_width), 'exper...  10.1 us
    all_to_all x1, starting transfers between devices, on_device(): lax.all_to_all(routed, 'expert', split_axis=0, concat_axis=0, tiled=True)  9.91 us
    all_to_all x1, waiting for transfers between devices, on_device(): lax.all_to_all(routed, 'expert', split_axis=0, concat_axis=0, tiled=True)  8.18 us
    all_to_all x1, waiting for transfers between devices, on_device(): lax.all_to_all(inputs, 'expert', split_axis=0, concat_axis=0, tiled=True)  5.62 us
  transfers between devices with their start and end apart: 5, of which 4 were waited for; matrix products, arithmetic and copies ran while one was open for 5% of the time, Pallas kernels for 0%

commit v1 on v0

v1 whole, which is shorter than its diff:
```python
import jax
import jax.numpy as jnp
from jax import lax
from jax.experimental import pallas as pl
from jax.experimental.pallas import tpu as pltpu
from jax.sharding import PartitionSpec as P

CAP = 16
PLANE = 32
EARLY_PARTS = 8
LATE_PARTS = 4


step_size = 2.0
mix_share = 0.5

f32 = jnp.float32
bf16 = jnp.bfloat16


def place(y, x, core):
    return (y * 4 + x) * 2 + core


LAST = place(3, 3, 1)
HELPERS = (
    place(3, 0, 0),
    place(0, 3, 1),
    place(0, 0, 1),
    place(3, 2, 0),
    place(2, 3, 0),
    place(0, 1, 1),
    place(1, 0, 1),
)


def times(left, right, left_dim=1, right_dim=0):
    return lax.dot_general(
        left, right, (((left_dim,), (right_dim,)), ((), ())), preferred_element_type=f32
    )


def pick_kernel(ids, gates, tokens, cotangent, sent, shares, picks):
    experts = sent.shape[0]
    count = tokens.shape[0]
    all_ids, all_gates = ids[...], gates[...]
    named_rows, share_rows = [], []
    for e in range(experts):
        hits = all_ids == e
        named_rows.append(jnp.max(hits.astype(f32), axis=0, keepdims=True))
        share_rows.append(jnp.sum(jnp.where(hits, all_gates, 0.0), axis=0, keepdims=True))
    named = jnp.concatenate(named_rows, axis=0)
    before = (
        lax.broadcasted_iota(jnp.int32, (count, count), 0)
        <= lax.broadcasted_iota(jnp.int32, (count, count), 1)
    ).astype(bf16)
    position = jnp.where(named > 0.0, times(named.astype(bf16), before), 0.0).astype(jnp.int32)
    slot = lax.broadcasted_iota(jnp.int32, (CAP, count), 0) + 1
    picked = jnp.concatenate(
        [jnp.broadcast_to(position[e : e + 1], (CAP, count)) == slot for e in range(experts)],
        axis=0,
    )
    share = jnp.concatenate(
        [jnp.broadcast_to(share_rows[e], (CAP, count)) for e in range(experts)], axis=0
    )
    share = jnp.where(picked, share, 0.0)
    shares[...] = share
    picked = picked.astype(bf16)
    picks[...] = picked
    slot_share = jnp.sum(share, axis=1, keepdims=True)
    width = tokens.shape[1]
    rows = (experts, CAP, width)
    sent[:, :CAP, :] = times(picked, tokens[...]).astype(bf16).reshape(rows)
    sent[:, CAP:, :] = (slot_share * times(picked, cotangent[...])).astype(bf16).reshape(rows)


def expert_kernel(arrived, project, weights, back, factors, *parts):
    sources = arrived.shape[0]
    width = arrived.shape[2]
    hidden_width = weights.shape[0]
    scale = hidden_width ** (-0.5)
    rows = (sources * CAP, width)
    inputs = arrived[:, :CAP, :].reshape(rows)
    routed = arrived[:, CAP:, :].reshape(rows)
    gate_pre = times(inputs, project[:, :hidden_width])
    up_pre = times(inputs, project[:, hidden_width:])
    sigmoid_value = jax.nn.sigmoid(gate_pre)
    activated = gate_pre * sigmoid_value
    hidden = (activated * up_pre).astype(bf16)
    factors[:, :hidden_width] = hidden
    factors[:, hidden_width:] = routed
    height = rows[0] // len(parts)
    for k, part in enumerate(parts):
        part[:, :hidden_width] = hidden[k * height : (k + 1) * height]
        part[:, hidden_width:] = routed[k * height : (k + 1) * height]
    block = (sources, CAP, width)
    back[:, :CAP, :] = (times(hidden, weights[...]) * scale).astype(bf16).reshape(block)
    hidden_grad = times(routed, weights[...], 1, 1) * scale
    slope = sigmoid_value * (1.0 + gate_pre * (1.0 - sigmoid_value))
    gate_grad = (hidden_grad * up_pre * slope).astype(bf16)
    up_grad = (hidden_grad * activated).astype(bf16)
    input_grad = times(gate_grad, project[:, :hidden_width], 1, 1) + times(
        up_grad, project[:, hidden_width:], 1, 1
    )
    back[:, CAP:, :] = input_grad.astype(bf16).reshape(block)


def combine_kernel(came_back, shares, picks, layer_out, token_grad):
    experts = came_back.shape[0]
    rows = (experts * CAP, came_back.shape[2])
    share = shares[...]
    upper = share.astype(bf16)
    lower = (share - upper.astype(f32)).astype(bf16)
    outputs = came_back[:, :CAP, :].reshape(rows)
    layer_out[...] = (times(upper, outputs, 0, 0) + times(lower, outputs, 0, 0)).astype(bf16)
    token_grad[...] = times(picks[...], came_back[:, CAP:, :].reshape(rows), 0, 0).astype(bf16)


def stepped(weights, factors):
    hidden_width = weights.shape[0]
    weight_grad = times(factors[:, :hidden_width], factors[:, hidden_width:], 0, 0) * (
        hidden_width ** (-0.5)
    )
    return (weights.astype(f32) - step_size * weight_grad).astype(bf16)


def step_kernel(weights, factors, updated):
    updated[...] = stepped(weights[...], factors[...])


def mix_kernel(first, updated, near_weights, near_factors, *rest):
    far_weights = rest[:EARLY_PARTS]
    far_factors = rest[EARLY_PARTS : EARLY_PARTS + LATE_PARTS]
    mixed, held_weights, held_factors = rest[EARLY_PARTS + LATE_PARTS :]

    @pl.when(first[0] == 1)
    def _():
        for held, parts in ((held_weights, far_weights), (held_factors, far_factors)):
            height = held.shape[0] // len(parts)
            for k, part in enumerate(parts):
                held[k * height : (k + 1) * height, :] = part[...]

    @pl.when(first[0] != 1)
    def _():
        held_weights[...] = near_weights[...]
        held_factors[...] = near_factors[...]

    neighbor = stepped(held_weights[...], held_factors[...])
    mixed[...] = (
        (1.0 - mix_share) * updated[...].astype(f32) + mix_share * neighbor.astype(f32)
    ).astype(bf16)


def shape(dims, dtype=bf16):
    return jax.ShapeDtypeStruct(dims, dtype)


VMEM = pl.BlockSpec(memory_space=pltpu.VMEM)


def pick(ids, gates, tokens, cotangent, experts):
    count, width = tokens.shape
    return pl.pallas_call(
        pick_kernel,
        out_shape=(
            shape((experts, 2 * CAP, width)),
            shape((experts * CAP, count), f32),
            shape((experts * CAP, count)),
        ),
        name="pick",
    )(ids, gates, tokens, cotangent)


def expert_pass(arrived, project, weights):
    rows = arrived.shape[0] * CAP
    columns = weights.shape[0] + weights.shape[1]
    return pl.pallas_call(
        expert_kernel,
        out_shape=(shape(arrived.shape), shape((rows, columns)))
        + (shape((rows // LATE_PARTS, columns)),) * LATE_PARTS,
        name="expert_pass",
    )(arrived, project, weights)


def combine(came_back, shares, picks):
    count = shares.shape[1]
    width = came_back.shape[2]
    return pl.pallas_call(
        combine_kernel,
        out_shape=(shape((count, width)), shape((count, width))),
        name="combine",
    )(came_back, shares, picks)


def step(weights, factors):
    return pl.pallas_call(step_kernel, out_shape=shape(weights.shape), name="step")(
        weights, factors
    )


def mix(first, updated, near_weights, far_weights, near_factors, far_factors):
    whole = [VMEM] * (3 + len(far_weights) + len(far_factors))
    return pl.pallas_call(
        mix_kernel,
        out_shape=shape(updated.shape),
        in_specs=[pl.BlockSpec(memory_space=pltpu.SMEM)] + whole,
        out_specs=VMEM,
        scratch_shapes=[
            pltpu.VMEM(near_weights.shape, bf16),
            pltpu.VMEM(near_factors.shape, bf16),
        ],
        name="mix",
    )(first, updated, near_weights, near_factors, *far_weights, *far_factors)


def from_previous(array, pieces):
    replicas = lax.axis_size("replica")
    planes = [h * PLANE for h in range(replicas // PLANE)]
    held = [pieces[0]]
    for k, piece in enumerate(pieces[1:]):
        route = [(h + LAST, h + HELPERS[k]) for h in planes]
        held.append(lax.ppermute(piece, "replica", route))
    route = [(h + i, h + i + 1) for h in planes for i in range(PLANE - 1)]
    near = lax.ppermute(array, "replica", route)
    far = []
    for source, piece in zip((LAST,) + HELPERS, held):
        route = [(h + source, (h + PLANE) % replicas) for h in planes]
        far.append(lax.ppermute(piece, "replica", route))
    return near, far


def on_device(tokens, cotangent, expert_ids, gate_weights, gate_up, down_weights):
    experts = lax.axis_size("expert")
    weights = down_weights[0, 0]
    project = gate_up[0]
    sent, shares, picks = pick(expert_ids.T, gate_weights.T, tokens, cotangent, experts)
    arrived = lax.all_to_all(sent, "expert", split_axis=0, concat_axis=0, tiled=True)
    height = weights.shape[0] // EARLY_PARTS
    pieces = [weights[k * height : (k + 1) * height] for k in range(EARLY_PARTS)]
    near_weights, far_weights = from_previous(weights, pieces)
    back, factors, *parts = expert_pass(arrived, project, weights)
    came_back = lax.all_to_all(back, "expert", split_axis=0, concat_axis=0, tiled=True)
    near_factors, far_factors = from_previous(factors, parts)
    updated = step(weights, factors)
    first = (lax.axis_index("replica") % PLANE == 0).astype(jnp.int32).reshape(1)
    mixed = mix(first, updated, near_weights, far_weights, near_factors, far_factors)
    layer_out, token_grad = combine(came_back, shares, picks)
    return (layer_out, token_grad, mixed[None, None])


def solution(mesh):
    return jax.shard_map(
        on_device,
        mesh=mesh,
        in_specs=(
            P(("replica", "expert"), None),
            P(("replica", "expert"), None),
            P(("replica", "expert"), None),
            P(("replica", "expert"), None),
            P("expert", None, None),
            P("replica", "expert", None, None),
        ),
        out_specs=(
            P(("replica", "expert"), None),
            P(("replica", "expert"), None),
            P("replica", "expert", None, None),
        ),
        check_vma=False,
    )
```

time: 205 us -> 174 us (0.85)
  the two profiles are of different devices: /device:TPU:128 before, /device:TPU:96 now
where the time goes in v1:
time: 174 us; the launch traced here: 173 us
  waiting for transfers between devices  82 us (47%)
  blocking collectives  36.1 us (21%)
  starting transfers between devices  35.6 us (20%)
  Pallas kernels  15.9 us (9%)
  local copies, waits for them, and re-layouts  2.39 us (1%)
    ppermute x12, waiting for transfers between devices, from_previous(): far.append(lax.ppermute(piece, 'replica', route))  82 us
    all_to_all x1, blocking collectives, on_device(): lax.all_to_all(sent, 'expert', split_axis=0, concat_axis=0, tiled=True)  36.1 us
    ppermute x12, starting transfers between devices, from_previous(): far.append(lax.ppermute(piece, 'replica', route))  15.5 us
    all_to_all x1, starting transfers between devices, on_device(): lax.all_to_all(back, 'expert', split_axis=0, concat_axis=0, tiled=True)  8.82 us
    ppermute x10, starting transfers between devices, from_previous(): held.append(lax.ppermute(piece, 'replica', route))  8.53 us
    pallas_call x1, Pallas kernels, expert_pass(): pl.pallas_call(expert_kernel, out_shape=(shape(arrived.shape), shape((row...  4.69 us
    pallas_call x1, Pallas kernels, mix(): pl.pallas_call(mix_kernel, out_shape=shape(updated.shape), in_specs=[pl.B...  3.95 us
  transfers between devices with their start and end apart: 25, of which 5 were waited for; matrix products, arithmetic and copies ran while one was open for 0% of the time, Pallas kernels for 4%

profile of v1, /device:TPU:96, one launch (start us, length us, event | category | flops | bytes accessed | tf_op | source)
XLA Modules:
  0.0 173.1 jit_solution(9917302298652982857)
XLA Ops:
  0.6 2.3 %pick.1 = (bf16[8,32,1024]{2,1,0:T(8,128)(2,1)}, f32[128,128]{1,0:T(8,128)}, bf16[128,128]{1,0:T(8,128)(2,1)}) custom-call(s32[8,128]{1,0:T(8,128)} %bitcast.27, f32[8,128]{1,0:T(8,128)} %bitcast.28, bf16[128,1024]{1,0:T(8,128)(2,1)} %tokens.1, bf16[128,1024]{1,0:T(8,128)(2,1)} %cotangent.1), custom_call_target="tpu_custom_call" | custom-call | tf_op jit(solution)/shard_map/pick/pallas_call | solution.py:163
  2.9 36.1 %all_to_all.10.arrived = bf16[8,32,1024]{2,1,0:T(8,128)(2,1)} all-to-all(bf16[8,32,1024]{2,1,0:T(8,128)(2,1)} %get-tuple-element.14), channel_id=1, replica_groups=mesh['replica'=128,'expert'=8] {'expert'}, dimensions={0} | all-to-all | bytes 1048576 | tf_op jit(solution)/shard_map/all_to_all | solution.py:237
  39.0 4.7 %expert_pass.1 = (bf16[8,32,1024]{2,1,0:T(8,128)(2,1)}, bf16[128,1536]{1,0:T(8,128)(2,1)}, bf16[32,1536]{1,0:T(8,128)(2,1)}, bf16[32,1536]{1,0:T(8,128)(2,1)}, b...) custom-call(bf16[8,32,1024]{2,1,0:T(8,128)(2,1)} %all_to_all.10.arrived, bf16[1024,1024]{1,0:T(8,128)(2,1)} %bitcast.25, ...), custom_call_target="tpu_custom_call" | custom-call | tf_op jit(solution)/shard_map/expert_pass/pallas_call | solution.py:177
  43.7 8.8 %all-to-all-start.1 = ((bf16[8,32,1024]{2,1,0:T(8,128)(2,1)}), bf16[8,32,1024]{2,1,0:T(8,128)(2,1)S(1)}, u32[]{:S(2)}, u32[]{:S(2)}) async-start(bf16[8,32,1024]{2,1,0:T(8,128)(2,1)} %get-tuple-element.15), calls=%async_computation.1 | async-start | bytes 1048576 | tf_op jit(solution)/shard_map/all_to_all | solution.py:242
  52.6 1.5 collective-permute-start
  54.1 0.1 slice_bitcast_fusion
  54.2 0.7 collective-permute-start.15
  54.8 0.7 collective-permute-start.11
  55.5 0.7 collective-permute-start.9
  56.2 0.7 collective-permute-start.7
  56.9 0.0 collective-permute-done.15
  56.9 0.7 collective-permute-start.5
  57.6 0.7 collective-permute-start.3
  58.2 0.0 collective-permute-done.9
  58.2 1.3 collective-permute-start.2
  59.5 0.0 collective-permute-done.7
  59.6 0.7 collective-permute-start.13
  60.2 1.3 collective-permute-start.16
  61.5 0.0 collective-permute-done.3
  61.6 1.3 collective-permute-start.12
  62.9 41.6 %collective-permute-done.2.rest_0_ = bf16[64,1024]{1,0:T(8,128)(2,1)S(1)} collective-permute-done((bf16[64,1024]{1,0:T(8,128)(2,1)S(1)}, bf16[64,1024]{1,0:T(8,128)(2,1)S(1)}, u32[]{:S(2)}, u32[]{:S(2)}) %collective-permute-start.2) | collective-permute-done | bytes 131104 | tf_op jit(solution)/shard_map/ppermute | solution.py:228
  104.4 1.3 collective-permute-start.10
  105.7 1.3 collective-permute-start.8
  107.1 0.6 copy-done.6
  107.7 1.3 collective-permute-start.1
  109.0 1.3 collective-permute-start.6
  110.3 14.5 %collective-permute-done.10.rest_4_ = bf16[64,1024]{1,0:T(8,128)(2,1)S(1)} collective-permute-done((bf16[64,1024]{1,0:T(8,128)(2,1)S(1)}, bf16[64,1024]{1,0:T(8,128)(2,1)S(1)}, u32[]{:S(2)}, u32[]{:S(2)}) %collective-permute-start.10) | collective-permute-done | bytes 131104 | tf_op jit(solution)/shard_map/ppermute | solution.py:228
  124.9 1.3 collective-permute-start.4
  126.2 1.3 collective-permute-start.14
  127.5 3.5 %collective-permute-done.6.rest_2_ = bf16[64,1024]{1,0:T(8,128)(2,1)S(1)} collective-permute-done((bf16[64,1024]{1,0:T(8,128)(2,1)S(1)}, bf16[64,1024]{1,0:T(8,128)(2,1)S(1)}, u32[]{:S(2)}, u32[]{:S(2)}) %collective-permute-start.6) | collective-permute-done | bytes 131104 | tf_op jit(solution)/shard_map/ppermute | solution.py:228
  131.0 1.3 collective-permute-start.18
  132.3 10.5 %collective-permute-done.4.rest_1_ = bf16[64,1024]{1,0:T(8,128)(2,1)S(1)} collective-permute-done((bf16[64,1024]{1,0:T(8,128)(2,1)S(1)}, bf16[64,1024]{1,0:T(8,128)(2,1)S(1)}, u32[]{:S(2)}, u32[]{:S(2)}) %collective-permute-start.4) | collective-permute-done | bytes 131104 | tf_op jit(solution)/shard_map/ppermute | solution.py:228
  142.8 1.3 collective-permute-start.20
  144.0 1.3 collective-permute-start.22
  145.3 1.3 collective-permute-start.17
  146.7 1.3 collective-permute-start.19
  148.0 1.3 collective-permute-start.21
  149.3 1.3 collective-permute-start.23
  150.6 2.8 %step.1.updated = bf16[512,1024]{1,0:T(8,128)(2,1)} custom-call(bf16[512,1024]{1,0:T(8,128)(2,1)} %bitcast.23, bf16[128,1536]{1,0:T(8,128)(2,1)} %get-tuple-element.20.factors), custom_call_target="tpu_custom_call" | custom-call | tf_op jit(solution)/shard_map/step/pallas_call | solution.py:196
  153.4 11.8 %collective-permute-done.17.rest_8_ = bf16[32,1536]{1,0:T(8,128)(2,1)S(1)} collective-permute-done((bf16[32,1536]{1,0:T(8,128)(2,1)}, bf16[32,1536]{1,0:T(8,128)(2,1)S(1)}, u32[]{:S(2)}, u32[]{:S(2)}) %collective-permute-start.17) | collective-permute-done | bytes 98336 | tf_op jit(solution)/shard_map/ppermute | solution.py:228
  165.4 0.6 copy-done.13
  165.9 0.1 copy-done.14
  166.0 0.0 copy-done.15
  166.0 0.0 copy-done.16
  166.0 0.1 copy-done.4
  166.2 4.0 %mix.1 = bf16[512,1024]{1,0:T(8,128)(2,1)} custom-call(s32[1]{0:T(128)} %bitcast.4.first, bf16[512,1024]{1,0:T(8,128)(2,1)} %step.1.updated, bf16[512,1024]{1,0:T(8,128)(2,1)} %copy-done.2, bf16[128,1536]{1,0:T(8,128)(2,1)} %copy-done.4, bf16[64,1024]{1,0:T(8,128)(2,1)} %copy-done.5, bf16[64,1024]{1,0:T(8,128)(2,1)} %copy-done.11, ...), custom_call_target="tpu_custom_call" | custom-call | tf_op jit(solution)/shard_map/mix/pallas_call | solution.py:203
  170.1 0.8 copy-done.1
  170.9 2.2 %combine.1 = (bf16[128,1024]{1,0:T(8,128)(2,1)}, bf16[128,1024]{1,0:T(8,128)(2,1)}) custom-call(bf16[8,32,1024]{2,1,0:T(8,128)(2,1)} %copy-done.1, f32[128,128]{1,0:T(8,128)} %get-tuple-element.16.shares, bf16[128,128]{1,0:T(8,128)(2,1)} %get-tuple-element.17.picks), custom_call_target="tpu_custom_call" | custom-call | tf_op jit(solution)/shard_map/combine/pallas_call | solution.py:188
  (49 shorter events, 0.1 us)
Async XLA Ops:
  39.0 13.5 %copy-start = (bf16[1,1,512,1024]{3,2,1,0:T(8,128)(2,1)S(1)}, bf16[1,1,512,1024]{3,2,1,0:T(8,128)(2,1)}, u32[]{:S(2)}) copy-start(bf16[1,1,512,1024]{3,2,1,0:T(8,128)(2,1)} %param.11) | copy-start | bytes 3145732
  43.7 64.0 %copy-start.3 = (bf16[128,1536]{1,0:T(8,128)(2,1)S(1)}, bf16[128,1536]{1,0:T(8,128)(2,1)}, u32[]{:S(2)}) copy-start(bf16[128,1536]{1,0:T(8,128)(2,1)} %get-tuple-element.20.factors) | copy-start | bytes 1179652
  43.7 126.4 %all-to-all-start.1 = ((bf16[8,32,1024]{2,1,0:T(8,128)(2,1)}), bf16[8,32,1024]{2,1,0:T(8,128)(2,1)S(1)}, u32[]{:S(2)}, u32[]{:S(2)}) async-start(bf16[8,32,1024]{2,1,0:T(8,128)(2,1)} %get-tuple-element.15), calls=%async_computation.1 | async-start | bytes 1048576 | tf_op jit(solution)/shard_map/all_to_all | solution.py:242
  52.6 78.4 %copy-start.19 = (bf16[32,1536]{1,0:T(8,128)(2,1)S(1)}, bf16[32,1536]{1,0:T(8,128)(2,1)}, u32[]{:S(2)}) copy-start(bf16[32,1536]{1,0:T(8,128)(2,1)} %get-tuple-element.22) | copy-start | bytes 294916
  52.6 90.2 %copy-start.18 = (bf16[32,1536]{1,0:T(8,128)(2,1)S(1)}, bf16[32,1536]{1,0:T(8,128)(2,1)}, u32[]{:S(2)}) copy-start(bf16[32,1536]{1,0:T(8,128)(2,1)} %get-tuple-element.23) | copy-start | bytes 294916
  52.6 91.5 %copy-start.17 = (bf16[32,1536]{1,0:T(8,128)(2,1)S(1)}, bf16[32,1536]{1,0:T(8,128)(2,1)}, u32[]{:S(2)}) copy-start(bf16[32,1536]{1,0:T(8,128)(2,1)} %get-tuple-element.24) | copy-start | bytes 294916
  52.6 92.8 %collective-permute-start = (bf16[512,1024]{1,0:T(8,128)(2,1)S(1)}, bf16[512,1024]{1,0:T(8,128)(2,1)S(1)}, u32[]{:S(2)}, u32[]{:S(2)}) collective-permute-start(bf16[512,1024]{1,0:T(8,128)(2,1)S(1)} %bitcast.24), channel_id=1, source_target_pairs={{0,8},{8,16},{16,24},{24,32},{32,40},{40,48},{48,56},{56,64},{64,7... | collective-permute-start | bytes 3145736 | tf_op jit(solution)/shard_map/ppermute | solution.py:224
  54.2 2.7 %collective-permute-start.15 = (bf16[64,1024]{1,0:T(8,128)(2,1)S(1)}, bf16[64,1024]{1,0:T(8,128)(2,1)S(1)}, u32[]{:S(2)}, u32[]{:S(2)}) collective-permute-start(bf16[64,1024]{1,0:T(8,128)(2,1)S(1)} %get-tuple-element.25), channel_id=1, source_target_pairs={{248,72},{504,328},{760,584},{1016,840},{249,73},{505,329},{761,58... | collective-permute-start | bytes 393224 | tf_op jit(solution)/shard_map/ppermute | solution.py:222
  54.8 2.7 %collective-permute-start.11 = (bf16[64,1024]{1,0:T(8,128)(2,1)S(1)}, bf16[64,1024]{1,0:T(8,128)(2,1)S(1)}, u32[]{:S(2)}, u32[]{:S(2)}) collective-permute-start(bf16[64,1024]{1,0:T(8,128)(2,1)S(1)} %get-tuple-element.26), channel_id=1, source_target_pairs={{248,176},{504,432},{760,688},{1016,944},{249,177},{505,433},{761,... | collective-permute-start | bytes 393224 | tf_op jit(solution)/shard_map/ppermute | solution.py:222
  55.5 2.7 %collective-permute-start.9 = (bf16[64,1024]{1,0:T(8,128)(2,1)S(1)}, bf16[64,1024]{1,0:T(8,128)(2,1)S(1)}, u32[]{:S(2)}, u32[]{:S(2)}) collective-permute-start(bf16[64,1024]{1,0:T(8,128)(2,1)S(1)} %get-tuple-element.27), channel_id=1, source_target_pairs={{248,224},{504,480},{760,736},{1016,992},{249,225},{505,481},{761,... | collective-permute-start | bytes 393224 | tf_op jit(solution)/shard_map/ppermute | solution.py:222
  56.2 3.4 %collective-permute-start.7 = (bf16[64,1024]{1,0:T(8,128)(2,1)S(1)}, bf16[64,1024]{1,0:T(8,128)(2,1)S(1)}, u32[]{:S(2)}, u32[]{:S(2)}) collective-permute-start(bf16[64,1024]{1,0:T(8,128)(2,1)S(1)} %get-tuple-element.28), channel_id=1, source_target_pairs={{248,8},{504,264},{760,520},{1016,776},{249,9},{505,265},{761,521}... | collective-permute-start | bytes 393224 | tf_op jit(solution)/shard_map/ppermute | solution.py:222
  56.9 3.4 %collective-permute-start.5 = (bf16[64,1024]{1,0:T(8,128)(2,1)S(1)}, bf16[64,1024]{1,0:T(8,128)(2,1)S(1)}, u32[]{:S(2)}, u32[]{:S(2)}) collective-permute-start(bf16[64,1024]{1,0:T(8,128)(2,1)S(1)} %get-tuple-element.29), channel_id=1, source_target_pairs={{248,56},{504,312},{760,568},{1016,824},{249,57},{505,313},{761,56... | collective-permute-start | bytes 393224 | tf_op jit(solution)/shard_map/ppermute | solution.py:222
  57.6 4.0 %collective-permute-start.3 = (bf16[64,1024]{1,0:T(8,128)(2,1)S(1)}, bf16[64,1024]{1,0:T(8,128)(2,1)S(1)}, u32[]{:S(2)}, u32[]{:S(2)}) collective-permute-start(bf16[64,1024]{1,0:T(8,128)(2,1)S(1)} %get-tuple-element.30), channel_id=1, source_target_pairs={{248,192},{504,448},{760,704},{1016,960},{249,193},{505,449},{761,... | collective-permute-start | bytes 393224 | tf_op jit(solution)/shard_map/ppermute | solution.py:222
  58.2 46.2 %collective-permute-start.2 = (bf16[64,1024]{1,0:T(8,128)(2,1)S(1)}, bf16[64,1024]{1,0:T(8,128)(2,1)S(1)}, u32[]{:S(2)}, u32[]{:S(2)}) collective-permute-start(bf16[64,1024]{1,0:T(8,128)(2,1)S(1)} %get-tuple-element.31), channel_id=1, source_target_pairs={{248,256},{504,512},{760,768},{1016,0},{249,257},{505,513},{761,76... | collective-permute-start | bytes 393224 | tf_op jit(solution)/shard_map/ppermute | solution.py:228
  59.6 46.2 %collective-permute-start.13 = (bf16[64,1024]{1,0:T(8,128)(2,1)S(1)}, bf16[64,1024]{1,0:T(8,128)(2,1)S(1)}, u32[]{:S(2)}, u32[]{:S(2)}) collective-permute-start(bf16[64,1024]{1,0:T(8,128)(2,1)S(1)} %get-tuple-element.32), channel_id=1, source_target_pairs={{248,24},{504,280},{760,536},{1016,792},{249,25},{505,281},{761,53... | collective-permute-start | bytes 393224 | tf_op jit(solution)/shard_map/ppermute | solution.py:222
  60.2 46.8 %collective-permute-start.16 = (bf16[64,1024]{1,0:T(8,128)(2,1)S(1)}, bf16[64,1024]{1,0:T(8,128)(2,1)S(1)}, u32[]{:S(2)}, u32[]{:S(2)}) collective-permute-start(bf16[64,1024]{1,0:T(8,128)(2,1)S(1)} %collective-permute-done.15), channel_id=1, source_target_pairs={{72,256},{328,512},{584,768},{840,0},{73,257},{329,513},{585,769},... | collective-permute-start | bytes 393224 | tf_op jit(solution)/shard_map/ppermute | solution.py:228
  61.6 47.5 %collective-permute-start.12 = (bf16[64,1024]{1,0:T(8,128)(2,1)S(1)}, bf16[64,1024]{1,0:T(8,128)(2,1)S(1)}, u32[]{:S(2)}, u32[]{:S(2)}) collective-permute-start(bf16[64,1024]{1,0:T(8,128)(2,1)S(1)} %collective-permute-done.11), channel_id=1, source_target_pairs={{176,256},{432,512},{688,768},{944,0},{177,257},{433,513},{689,769... | collective-permute-start | bytes 393224 | tf_op jit(solution)/shard_map/ppermute | solution.py:228
  104.4 60.9 %copy-start.5 = (bf16[64,1024]{1,0:T(8,128)(2,1)}, bf16[64,1024]{1,0:T(8,128)(2,1)S(1)}, u32[]{:S(2)}) copy-start(bf16[64,1024]{1,0:T(8,128)(2,1)S(1)} %collective-permute-done.2.rest_0_) | copy-start | bytes 393220
  104.4 20.4 %collective-permute-start.10 = (bf16[64,1024]{1,0:T(8,128)(2,1)S(1)}, bf16[64,1024]{1,0:T(8,128)(2,1)S(1)}, u32[]{:S(2)}, u32[]{:S(2)}) collective-permute-start(bf16[64,1024]{1,0:T(8,128)(2,1)S(1)} %collective-permute-done.9), channel_id=1, source_target_pairs={{224,256},{480,512},{736,768},{992,0},{225,257},{481,513},{737,769... | collective-permute-start | bytes 393224 | tf_op jit(solution)/shard_map/ppermute | solution.py:228
  105.7 20.4 %collective-permute-start.8 = (bf16[64,1024]{1,0:T(8,128)(2,1)S(1)}, bf16[64,1024]{1,0:T(8,128)(2,1)S(1)}, u32[]{:S(2)}, u32[]{:S(2)}) collective-permute-start(bf16[64,1024]{1,0:T(8,128)(2,1)S(1)} %collective-permute-done.7), channel_id=1, source_target_pairs={{8,256},{264,512},{520,768},{776,0},{9,257},{265,513},{521,769},{7... | collective-permute-start | bytes 393224 | tf_op jit(solution)/shard_map/ppermute | solution.py:228
  107.0 0.6 copy-start.6
  107.7 57.6 %collective-permute-start.1 = (bf16[128,1536]{1,0:T(8,128)(2,1)S(1)}, bf16[128,1536]{1,0:T(8,128)(2,1)S(1)}, u32[]{:S(2)}, u32[]{:S(2)}) collective-permute-start(bf16[128,1536]{1,0:T(8,128)(2,1)S(1)} %copy-done.3), channel_id=1, source_target_pairs={{0,8},{8,16},{16,24},{24,32},{32,40},{40,48},{48,56},{56,64},{64,7... | collective-permute-start | bytes 1179656 | tf_op jit(solution)/shard_map/ppermute | solution.py:224
  109.0 36.3 %copy-start.7 = (bf16[64,1024]{1,0:T(8,128)(2,1)}, bf16[64,1024]{1,0:T(8,128)(2,1)S(1)}, u32[]{:S(2)}) copy-start(bf16[64,1024]{1,0:T(8,128)(2,1)S(1)} %collective-permute-done.12.rest_5_) | copy-start | bytes 393220
  109.0 21.9 %collective-permute-start.6 = (bf16[64,1024]{1,0:T(8,128)(2,1)S(1)}, bf16[64,1024]{1,0:T(8,128)(2,1)S(1)}, u32[]{:S(2)}, u32[]{:S(2)}) collective-permute-start(bf16[64,1024]{1,0:T(8,128)(2,1)S(1)} %collective-permute-done.5), channel_id=1, source_target_pairs={{56,256},{312,512},{568,768},{824,0},{57,257},{313,513},{569,769},... | collective-permute-start | bytes 393224 | tf_op jit(solution)/shard_map/ppermute | solution.py:228
  124.9 20.5 %copy-start.8 = (bf16[64,1024]{1,0:T(8,128)(2,1)}, bf16[64,1024]{1,0:T(8,128)(2,1)S(1)}, u32[]{:S(2)}) copy-start(bf16[64,1024]{1,0:T(8,128)(2,1)S(1)} %collective-permute-done.10.rest_4_) | copy-start | bytes 393220
  124.9 17.9 %collective-permute-start.4 = (bf16[64,1024]{1,0:T(8,128)(2,1)S(1)}, bf16[64,1024]{1,0:T(8,128)(2,1)S(1)}, u32[]{:S(2)}, u32[]{:S(2)}) collective-permute-start(bf16[64,1024]{1,0:T(8,128)(2,1)S(1)} %collective-permute-done.3), channel_id=1, source_target_pairs={{192,256},{448,512},{704,768},{960,0},{193,257},{449,513},{705,769... | collective-permute-start | bytes 393224 | tf_op jit(solution)/shard_map/ppermute | solution.py:228
  126.2 20.5 %copy-start.9 = (bf16[64,1024]{1,0:T(8,128)(2,1)}, bf16[64,1024]{1,0:T(8,128)(2,1)S(1)}, u32[]{:S(2)}) copy-start(bf16[64,1024]{1,0:T(8,128)(2,1)S(1)} %collective-permute-done.8.rest_3_) | copy-start | bytes 393220
  126.2 17.9 %collective-permute-start.14 = (bf16[64,1024]{1,0:T(8,128)(2,1)S(1)}, bf16[64,1024]{1,0:T(8,128)(2,1)S(1)}, u32[]{:S(2)}, u32[]{:S(2)}) collective-permute-start(bf16[64,1024]{1,0:T(8,128)(2,1)S(1)} %collective-permute-done.13), channel_id=1, source_target_pairs={{24,256},{280,512},{536,768},{792,0},{25,257},{281,513},{537,769},... | collective-permute-start | bytes 393224 | tf_op jit(solution)/shard_map/ppermute | solution.py:228
  131.0 15.7 %copy-start.10 = (bf16[64,1024]{1,0:T(8,128)(2,1)}, bf16[64,1024]{1,0:T(8,128)(2,1)S(1)}, u32[]{:S(2)}) copy-start(bf16[64,1024]{1,0:T(8,128)(2,1)S(1)} %collective-permute-done.6.rest_2_) | copy-start | bytes 393220
  131.0 15.7 %collective-permute-start.18 = (bf16[32,1536]{1,0:T(8,128)(2,1)S(1)}, bf16[32,1536]{1,0:T(8,128)(2,1)}, u32[]{:S(2)}, u32[]{:S(2)}) collective-permute-start(bf16[32,1536]{1,0:T(8,128)(2,1)S(1)} %copy-done.19), channel_id=1, source_target_pairs={{248,192},{504,448},{760,704},{1016,960},{249,193},{505,449},{761,... | collective-permute-start | bytes 294920 | tf_op jit(solution)/shard_map/ppermute | solution.py:222
  142.7 5.2 %copy-start.11 = (bf16[64,1024]{1,0:T(8,128)(2,1)}, bf16[64,1024]{1,0:T(8,128)(2,1)S(1)}, u32[]{:S(2)}) copy-start(bf16[64,1024]{1,0:T(8,128)(2,1)S(1)} %collective-permute-done.4.rest_1_) | copy-start | bytes 393220
  142.8 5.2 %collective-permute-start.20 = (bf16[32,1536]{1,0:T(8,128)(2,1)S(1)}, bf16[32,1536]{1,0:T(8,128)(2,1)}, u32[]{:S(2)}, u32[]{:S(2)}) collective-permute-start(bf16[32,1536]{1,0:T(8,128)(2,1)S(1)} %copy-done.18), channel_id=1, source_target_pairs={{248,56},{504,312},{760,568},{1016,824},{249,57},{505,313},{761,56... | collective-permute-start | bytes 294920 | tf_op jit(solution)/shard_map/ppermute | solution.py:222
  144.0 4.0 %copy-start.12 = (bf16[64,1024]{1,0:T(8,128)(2,1)}, bf16[64,1024]{1,0:T(8,128)(2,1)S(1)}, u32[]{:S(2)}) copy-start(bf16[64,1024]{1,0:T(8,128)(2,1)S(1)} %collective-permute-done.14.rest_6_) | copy-start | bytes 393220
  144.0 5.3 %collective-permute-start.22 = (bf16[32,1536]{1,0:T(8,128)(2,1)S(1)}, bf16[32,1536]{1,0:T(8,128)(2,1)}, u32[]{:S(2)}, u32[]{:S(2)}) collective-permute-start(bf16[32,1536]{1,0:T(8,128)(2,1)S(1)} %copy-done.17), channel_id=1, source_target_pairs={{248,8},{504,264},{760,520},{1016,776},{249,9},{505,265},{761,521}... | collective-permute-start | bytes 294920 | tf_op jit(solution)/shard_map/ppermute | solution.py:222
  145.3 20.0 %copy-start.2 = (bf16[512,1024]{1,0:T(8,128)(2,1)}, bf16[512,1024]{1,0:T(8,128)(2,1)S(1)}, u32[]{:S(2)}) copy-start(bf16[512,1024]{1,0:T(8,128)(2,1)S(1)} %collective-permute-done.near_weights) | copy-start | bytes 3145732
  145.3 19.9 %collective-permute-start.17 = (bf16[32,1536]{1,0:T(8,128)(2,1)}, bf16[32,1536]{1,0:T(8,128)(2,1)S(1)}, u32[]{:S(2)}, u32[]{:S(2)}) collective-permute-start(bf16[32,1536]{1,0:T(8,128)(2,1)} %get-tuple-element.21), channel_id=1, source_target_pairs={{248,256},{504,512},{760,768},{1016,0},{249,257},{505,513},{761,76... | collective-permute-start | bytes 294920 | tf_op jit(solution)/shard_map/ppermute | solution.py:228
  146.7 18.6 %collective-permute-start.19 = (bf16[32,1536]{1,0:T(8,128)(2,1)}, bf16[32,1536]{1,0:T(8,128)(2,1)S(1)}, u32[]{:S(2)}, u32[]{:S(2)}) collective-permute-start(bf16[32,1536]{1,0:T(8,128)(2,1)} %collective-permute-done.18), channel_id=1, source_target_pairs={{192,256},{448,512},{704,768},{960,0},{193,257},{449,513},{705,769... | collective-permute-start | bytes 294920 | tf_op jit(solution)/shard_map/ppermute | solution.py:228
  148.0 17.3 %collective-permute-start.21 = (bf16[32,1536]{1,0:T(8,128)(2,1)}, bf16[32,1536]{1,0:T(8,128)(2,1)S(1)}, u32[]{:S(2)}, u32[]{:S(2)}) collective-permute-start(bf16[32,1536]{1,0:T(8,128)(2,1)} %collective-permute-done.20), channel_id=1, source_target_pairs={{56,256},{312,512},{568,768},{824,0},{57,257},{313,513},{569,769},... | collective-permute-start | bytes 294920 | tf_op jit(solution)/shard_map/ppermute | solution.py:228
  149.3 16.0 %collective-permute-start.23 = (bf16[32,1536]{1,0:T(8,128)(2,1)}, bf16[32,1536]{1,0:T(8,128)(2,1)S(1)}, u32[]{:S(2)}, u32[]{:S(2)}) collective-permute-start(bf16[32,1536]{1,0:T(8,128)(2,1)} %collective-permute-done.22), channel_id=1, source_target_pairs={{8,256},{264,512},{520,768},{776,0},{9,257},{265,513},{521,769},{7... | collective-permute-start | bytes 294920 | tf_op jit(solution)/shard_map/ppermute | solution.py:228
  165.3 0.6 copy-start.13
  165.3 0.7 copy-start.14
  165.3 0.7 copy-start.15
  165.3 0.7 copy-start.16
  165.3 0.8 copy-start.4
  170.1 0.8 copy-start.1

commit v2 on v1

v2 whole, which is shorter than its diff:
```python
import jax
import jax.numpy as jnp
from jax import lax
from jax.experimental import pallas as pl
from jax.experimental.pallas import tpu as pltpu
from jax.sharding import PartitionSpec as P

CAP = 16
PLANE = 32


step_size = 2.0
mix_share = 0.5

f32 = jnp.float32
bf16 = jnp.bfloat16


def place(y, x, core):
    return (y * 4 + x) * 2 + core


LAST = place(3, 3, 1)
EARLY_FROM = (place(3, 2, 0), place(2, 3, 0), place(2, 1, 0), place(1, 2, 0))
LATE_FROM = (LAST, place(3, 0, 0), place(0, 3, 1), place(0, 0, 1))
EARLY_PARTS = len(EARLY_FROM)
LATE_PARTS = len(LATE_FROM)


def times(left, right, left_dim=1, right_dim=0):
    return lax.dot_general(
        left, right, (((left_dim,), (right_dim,)), ((), ())), preferred_element_type=f32
    )


def pick_kernel(ids_in, gates_in, tokens_in, cotangent_in, sent_out, shares_out, picks_out, *own):
    ids, gates, tokens, cotangent, sent, shares, picks, sems = own
    loads = [
        pltpu.make_async_copy(source, target, sems.at[k])
        for k, (source, target) in enumerate(
            ((ids_in, ids), (gates_in, gates), (tokens_in, tokens), (cotangent_in, cotangent))
        )
    ]
    for load in loads:
        load.start()
    experts = sent.shape[0]
    count, width = tokens.shape
    loads[0].wait()
    loads[1].wait()
    all_ids, all_gates = ids[...], gates[...]
    named_rows, share_rows = [], []
    for e in range(experts):
        hits = all_ids == e
        named_rows.append(jnp.max(hits.astype(f32), axis=0, keepdims=True))
        share_rows.append(jnp.sum(jnp.where(hits, all_gates, 0.0), axis=0, keepdims=True))
    named = jnp.concatenate(named_rows, axis=0)
    before = (
        lax.broadcasted_iota(jnp.int32, (count, count), 0)
        <= lax.broadcasted_iota(jnp.int32, (count, count), 1)
    ).astype(bf16)
    position = jnp.where(named > 0.0, times(named.astype(bf16), before), 0.0).astype(jnp.int32)
    slot = lax.broadcasted_iota(jnp.int32, (CAP, count), 0) + 1
    picked = jnp.concatenate(
        [jnp.broadcast_to(position[e : e + 1], (CAP, count)) == slot for e in range(experts)],
        axis=0,
    )
    share = jnp.concatenate(
        [jnp.broadcast_to(share_rows[e], (CAP, count)) for e in range(experts)], axis=0
    )
    share = jnp.where(picked, share, 0.0)
    shares[...] = share
    picked = picked.astype(bf16)
    picks[...] = picked
    rows = (experts, CAP, width)
    first, second = slice(0, CAP), slice(CAP, 2 * CAP)
    stores = [
        pltpu.make_async_copy(shares, shares_out, sems.at[4]),
        pltpu.make_async_copy(picks, picks_out, sems.at[5]),
        pltpu.make_async_copy(sent.at[:, first], sent_out.at[:, first], sems.at[6]),
        pltpu.make_async_copy(sent.at[:, second], sent_out.at[:, second], sems.at[7]),
    ]
    stores[0].start()
    stores[1].start()
    loads[2].wait()
    sent[:, first, :] = times(picked, tokens[...]).astype(bf16).reshape(rows)
    stores[2].start()
    slot_share = jnp.sum(share, axis=1, keepdims=True)
    loads[3].wait()
    sent[:, second, :] = (slot_share * times(picked, cotangent[...])).astype(bf16).reshape(rows)
    stores[3].start()
    for store in stores:
        store.wait()


def expert_kernel(arrived_in, project, weights, back_out, factors, *rest):
    parts, (arrived, back, sems) = rest[:LATE_PARTS], rest[LATE_PARTS:]
    sources, _, width = arrived.shape
    hidden_width = weights.shape[0]
    scale = hidden_width ** (-0.5)
    rows = (sources * CAP, width)
    block = (sources, CAP, width)
    halves = (slice(0, CAP), slice(CAP, 2 * CAP))
    loads = [
        pltpu.make_async_copy(arrived_in.at[:, half], arrived.at[:, half], sems.at[k])
        for k, half in enumerate(halves)
    ]
    for load in loads:
        load.start()
    height = rows[0] // len(parts)
    stores = [
        pltpu.make_async_copy(back.at[:, half], back_out.at[:, half], sems.at[2 + k])
        for k, half in enumerate(halves)
    ] + [
        pltpu.make_async_copy(factors.at[k * height : (k + 1) * height], part, sems.at[4 + k])
        for k, part in enumerate(parts)
    ]
    loads[0].wait()
    inputs = arrived[:, halves[0], :].reshape(rows)
    gate_pre = times(inputs, project[:, :hidden_width])
    up_pre = times(inputs, project[:, hidden_width:])
    sigmoid_value = jax.nn.sigmoid(gate_pre)
    activated = gate_pre * sigmoid_value
    hidden = (activated * up_pre).astype(bf16)
    factors[:, :hidden_width] = hidden
    loads[1].wait()
    routed = arrived[:, halves[1], :].reshape(rows)
    factors[:, hidden_width:] = routed
    for store in stores[2:]:
        store.start()
    back[:, halves[0], :] = (times(hidden, weights[...]) * scale).astype(bf16).reshape(block)
    stores[0].start()
    hidden_grad = times(routed, weights[...], 1, 1) * scale
    slope = sigmoid_value * (1.0 + gate_pre * (1.0 - sigmoid_value))
    gate_grad = (hidden_grad * up_pre * slope).astype(bf16)
    up_grad = (hidden_grad * activated).astype(bf16)
    input_grad = times(gate_grad, project[:, :hidden_width], 1, 1) + times(
        up_grad, project[:, hidden_width:], 1, 1
    )
    back[:, halves[1], :] = input_grad.astype(bf16).reshape(block)
    stores[1].start()
    for store in stores:
        store.wait()


def combine_kernel(came_back, shares, picks, layer_out, token_grad):
    experts = came_back.shape[0]
    rows = (experts * CAP, came_back.shape[2])
    share = shares[...]
    upper = share.astype(bf16)
    lower = (share - upper.astype(f32)).astype(bf16)
    outputs = came_back[:, :CAP, :].reshape(rows)
    layer_out[...] = (times(upper, outputs, 0, 0) + times(lower, outputs, 0, 0)).astype(bf16)
    token_grad[...] = times(picks[...], came_back[:, CAP:, :].reshape(rows), 0, 0).astype(bf16)


def stepped(weights, hidden, routed, hidden_width):
    weight_grad = times(hidden, routed, 0, 0) * (hidden_width ** (-0.5))
    return (weights.astype(f32) - step_size * weight_grad).astype(bf16)


def step_kernel(weights, factors, updated):
    hidden_width = weights.shape[0]
    updated[...] = stepped(
        weights[...], factors[:, :hidden_width], factors[:, hidden_width:], hidden_width
    )


def mix_kernel(first, updated, near, *rest):
    far_weights = rest[:EARLY_PARTS]
    far_factors = rest[EARLY_PARTS : EARLY_PARTS + LATE_PARTS]
    mixed, held_factors = rest[EARLY_PARTS + LATE_PARTS :]

    def put(rows, neighbor):
        mixed[rows, :] = (
            (1.0 - mix_share) * updated[rows, :].astype(f32) + mix_share * neighbor.astype(f32)
        ).astype(bf16)

    @pl.when(first[0] == 1)
    def _():
        height = held_factors.shape[0] // LATE_PARTS
        for k, part in enumerate(far_factors):
            held_factors[k * height : (k + 1) * height, :] = part[...]
        hidden_width = updated.shape[0]
        routed = held_factors[:, hidden_width:]
        height = hidden_width // EARLY_PARTS
        for k, part in enumerate(far_weights):
            rows = slice(k * height, (k + 1) * height)
            put(rows, stepped(part[...], held_factors[:, rows], routed, hidden_width))

    @pl.when(first[0] != 1)
    def _():
        put(slice(None), near[...])


def shape(dims, dtype=bf16):
    return jax.ShapeDtypeStruct(dims, dtype)


GRANT = pltpu.CompilerParams(vmem_limit_bytes=20 << 20)
HBM = pl.BlockSpec(memory_space=pltpu.HBM)
VMEM = pl.BlockSpec(memory_space=pltpu.VMEM)


def pick(ids, gates, tokens, cotangent, experts):
    count, width = tokens.shape
    outs = (
        shape((experts, 2 * CAP, width)),
        shape((experts * CAP, count), f32),
        shape((experts * CAP, count)),
    )
    ins = (ids, gates, tokens, cotangent)
    return pl.pallas_call(
        pick_kernel,
        out_shape=tuple(pltpu.HBM(x.shape, x.dtype) for x in outs),
        in_specs=[HBM] * len(ins),
        out_specs=[HBM] * len(outs),
        scratch_shapes=[pltpu.VMEM(x.shape, x.dtype) for x in ins + outs]
        + [pltpu.SemaphoreType.DMA((8,))],
        compiler_params=GRANT,
        name="pick",
    )(*(pltpu.with_memory_space_constraint(x, pltpu.HBM) for x in ins))


def expert_pass(arrived, project, weights):
    rows = arrived.shape[0] * CAP
    columns = weights.shape[0] + weights.shape[1]
    return pl.pallas_call(
        expert_kernel,
        out_shape=(pltpu.HBM(arrived.shape, bf16), shape((rows, columns)))
        + (pltpu.HBM((rows // LATE_PARTS, columns), bf16),) * LATE_PARTS,
        in_specs=[HBM, VMEM, VMEM],
        out_specs=[HBM, VMEM] + [HBM] * LATE_PARTS,
        scratch_shapes=[
            pltpu.VMEM(arrived.shape, bf16),
            pltpu.VMEM(arrived.shape, bf16),
            pltpu.SemaphoreType.DMA((4 + LATE_PARTS,)),
        ],
        compiler_params=GRANT,
        name="expert_pass",
    )(arrived, project, weights)


def combine(came_back, shares, picks):
    count = shares.shape[1]
    width = came_back.shape[2]
    return pl.pallas_call(
        combine_kernel,
        out_shape=(shape((count, width)), shape((count, width))),
        compiler_params=GRANT,
        name="combine",
    )(came_back, shares, picks)


def step(weights, factors):
    return pl.pallas_call(
        step_kernel, out_shape=shape(weights.shape), compiler_params=GRANT, name="step"
    )(weights, factors)


def mix(first, updated, near, far_weights, far_factors):
    rows, columns = far_factors[0].shape
    return pl.pallas_call(
        mix_kernel,
        out_shape=shape(updated.shape),
        in_specs=[pl.BlockSpec(memory_space=pltpu.SMEM)]
        + [VMEM] * (2 + len(far_weights) + len(far_factors)),
        out_specs=VMEM,
        scratch_shapes=[pltpu.VMEM((rows * LATE_PARTS, columns), bf16)],
        compiler_params=GRANT,
        name="mix",
    )(first, updated, near, *far_weights, *far_factors)


def planes_of():
    return range(0, lax.axis_size("replica"), PLANE)


def to_next(array):
    route = [(h + i, h + i + 1) for h in planes_of() for i in range(PLANE - 1)]
    return lax.ppermute(array, "replica", route)


def to_next_plane(pieces, places):
    held = []
    for piece, between in zip(pieces, places):
        if between == LAST:
            held.append(piece)
            continue
        route = [(h + LAST, h + between) for h in planes_of()]
        held.append(lax.ppermute(piece, "replica", route))
    far = []
    for piece, between in zip(held, places):
        route = [(h + between, (h + PLANE) % lax.axis_size("replica")) for h in planes_of()]
        far.append(lax.ppermute(piece, "replica", route))
    return far


def on_device(tokens, cotangent, expert_ids, gate_weights, gate_up, down_weights):
    experts = lax.axis_size("expert")
    weights = down_weights[0, 0]
    project = gate_up[0]
    sent, shares, picks = pick(expert_ids.T, gate_weights.T, tokens, cotangent, experts)
    arrived = lax.all_to_all(sent, "expert", split_axis=0, concat_axis=0, tiled=True)
    height = weights.shape[0] // EARLY_PARTS
    pieces = [weights[k * height : (k + 1) * height] for k in range(EARLY_PARTS)]
    far_weights = to_next_plane(pieces, EARLY_FROM)
    back, factors, *parts = expert_pass(arrived, project, weights)
    came_back = lax.all_to_all(back, "expert", split_axis=0, concat_axis=0, tiled=True)
    updated = step(weights, factors)
    far_factors = to_next_plane(parts, LATE_FROM)
    near = to_next(updated)
    first = (lax.axis_index("replica") % PLANE == 0).astype(jnp.int32).reshape(1)
    mixed = mix(first, updated, near, far_weights, far_factors)
    layer_out, token_grad = combine(came_back, shares, picks)
    return (layer_out, token_grad, mixed[None, None])


def solution(mesh):
    return jax.shard_map(
        on_device,
        mesh=mesh,
        in_specs=(
            P(("replica", "expert"), None),
            P(("replica", "expert"), None),
            P(("replica", "expert"), None),
            P(("replica", "expert"), None),
            P("expert", None, None),
            P("replica", "expert", None, None),
        ),
        out_specs=(
            P(("replica", "expert"), None),
            P(("replica", "expert"), None),
            P("replica", "expert", None, None),
        ),
        check_vma=False,
    )
```

time: 174 us -> 142 us (0.82)
  waiting for transfers between devices: 82 us -> 66.9 us
  starting transfers between devices: 35.6 us -> 26 us
  Pallas kernels: 15.9 us -> 9.67 us
    ppermute x24 -> x16, waiting for transfers between devices: 82 us -> 66.9 us  [the longest x8 66.9 us: to_next_plane(): far.append(lax.ppermute(piece, 'replica', route))]
    ppermute x24 -> x16, starting transfers between devices: 26.8 us -> 17.3 us  [the longest x8 10.3 us: to_next_plane(): far.append(lax.ppermute(piece, 'replica', route))]
    pallas_call x3, Pallas kernels: 9.77 us -> 5.45 us  [the longest x1 2.67 us: expert_pass(): pl.pallas_call(expert_kernel, out_shape=(pltpu.HBM(arrived.shape, bf16),...]
  transfers between devices with their start and end apart: 25 -> 17, of which waited for: 5 -> 3; matrix products, arithmetic and copies ran while one was open for 0% -> 0% of each run, Pallas kernels for 4% -> 3%
where the time goes in v2:
time: 142 us; the launch traced here: 141 us
  waiting for transfers between devices  66.9 us (47%)
  blocking collectives  36 us (25%)
  starting transfers between devices  26 us (18%)
  Pallas kernels  9.67 us (7%)
  local copies, waits for them, and re-layouts  1.69 us (1%)
    ppermute x8, waiting for transfers between devices, to_next_plane(): far.append(lax.ppermute(piece, 'replica', route))  66.9 us
    all_to_all x1, blocking collectives, on_device(): lax.all_to_all(sent, 'expert', split_axis=0, concat_axis=0, tiled=True)  36 us
    ppermute x8, starting transfers between devices, to_next_plane(): far.append(lax.ppermute(piece, 'replica', route))  10.3 us
    all_to_all x1, starting transfers between devices, on_device(): lax.all_to_all(back, 'expert', split_axis=0, concat_axis=0, tiled=True)  8.69 us
    ppermute x7, starting transfers between devices, to_next_plane(): held.append(lax.ppermute(piece, 'replica', route))  4.69 us
    pallas_call x1, Pallas kernels, mix(): pl.pallas_call(mix_kernel, out_shape=shape(updated.shape), in_specs=[pl.B...  3.1 us
  transfers between devices with their start and end apart: 17, of which 3 were waited for; matrix products, arithmetic and copies ran while one was open for 0% of the time, Pallas kernels for 3%

profile of v2, /device:TPU:96, one launch (start us, length us, event | category | flops | bytes accessed | tf_op | source)
XLA Modules:
  0.0 141.2 jit_solution(4121884324617752055)
XLA Ops:
  0.6 0.0 copy-start
  0.6 2.3 %pick.1 = (bf16[8,32,1024]{2,1,0:T(8,128)(2,1)}, f32[128,128]{1,0:T(8,128)}, bf16[128,128]{1,0:T(8,128)(2,1)}) custom-call(s32[8,128]{1,0:T(8,128)} %bitcast.18, f32[8,128]{1,0:T(8,128)} %bitcast.19, bf16[128,1024]{1,0:T(8,128)(2,1)} %tokens_in.1, bf16[128,1024]{1,0:T(8,128)(2,1)} %cotangent_in.1), custom_call_target="tpu_custom_call" | custom-call | tf_op jit(solution)/shard_map/pick/pallas_call | solution.py:212
  2.9 36.0 %all_to_all.10.arrived_in = bf16[8,32,1024]{2,1,0:T(8,128)(2,1)S(1)} all-to-all(bf16[8,32,1024]{2,1,0:T(8,128)(2,1)} %get-tuple-element.14), channel_id=1, replica_groups=mesh['replica'=128,'expert'=8] {'expert'}, dimensions={0} | all-to-all | bytes 1048576 | tf_op jit(solution)/shard_map/all_to_all | solution.py:303
  39.0 0.0 copy-done
  39.0 1.6 %copy-done.1 = bf16[1,1024,1024]{2,1,0:T(8,128)(2,1)S(1)} copy-done((bf16[1,1024,1024]{2,1,0:T(8,128)(2,1)S(1)}, bf16[1,1024,1024]{2,1,0:T(8,128)(2,1)}, u32[]{:S(2)}) %copy-start.1) | copy-done | bytes 2097176
  40.6 2.7 %expert_pass.1 = (bf16[8,32,1024]{2,1,0:T(8,128)(2,1)}, bf16[128,1536]{1,0:T(8,128)(2,1)S(1)}, bf16[32,1536]{1,0:T(8,128)(2,1)}, bf16[32,1536]{1,0:T(8,128)(2,1)...) custom-call(bf16[8,32,1024]{2,1,0:T(8,128)(2,1)S(1)} %all_to_all.10.arrived_in, bf16[1024,1024]{1,0:T(8,128)(2,1)S(1)} %bitcast.16, ...), custom_call_target="tpu_custom_call" | custom-call | tf_op jit(solution)/shard_map/expert_pass/pallas_call | solution.py:227
  43.3 8.7 %all-to-all-start.1 = ((bf16[8,32,1024]{2,1,0:T(8,128)(2,1)}), bf16[8,32,1024]{2,1,0:T(8,128)(2,1)S(1)}, u32[]{:S(2)}, u32[]{:S(2)}) async-start(bf16[8,32,1024]{2,1,0:T(8,128)(2,1)} %get-tuple-element.15), calls=%async_computation.1 | async-start | bytes 1048576 | tf_op jit(solution)/shard_map/all_to_all | solution.py:308
  52.0 0.0 copy-start.4
  52.0 0.5 step.1.updated
  52.5 2.3 %collective-permute-start = (bf16[512,1024]{1,0:T(8,128)(2,1)S(1)}, bf16[512,1024]{1,0:T(8,128)(2,1)}, u32[]{:S(2)}, u32[]{:S(2)}) collective-permute-start(bf16[512,1024]{1,0:T(8,128)(2,1)S(1)} %step.1.updated), channel_id=1, source_target_pairs={{0,8},{8,16},{16,24},{24,32},{32,40},{40,48},{48,56},{56,64},{64,7... | collective-permute-start | bytes 3145736 | tf_op jit(solution)/shard_map/ppermute | solution.py:280
  54.8 0.1 slice_bitcast_fusion
  54.8 0.7 collective-permute-start.7
  55.5 0.7 collective-permute-start.3
  56.2 0.7 collective-permute-start.1
  56.9 0.7 collective-permute-start.5
  57.6 0.0 collective-permute-done.7
  57.6 1.3 collective-permute-start.8
  58.9 0.0 collective-permute-done.3
  58.9 1.3 collective-permute-start.4
  60.2 0.0 collective-permute-done.1
  60.2 1.3 collective-permute-start.2
  61.5 0.0 collective-permute-done.5
  61.5 1.3 collective-permute-start.6
  62.8 50.7 %collective-permute-done.8.rest_3_ = bf16[128,1024]{1,0:T(8,128)(2,1)S(1)} collective-permute-done((bf16[128,1024]{1,0:T(8,128)(2,1)S(1)}, bf16[128,1024]{1,0:T(8,128)(2,1)S(1)}, u32[]{:S(2)}, u32[]{:S(2)}) %collective-permute-start.8) | collective-permute-done | bytes 262176 | tf_op jit(solution)/shard_map/ppermute | solution.py:294
  113.6 0.0 copy-done.7
  113.6 0.7 collective-permute-start.10
  114.2 1.7 %collective-permute-done.4.rest_1_ = bf16[128,1024]{1,0:T(8,128)(2,1)S(1)} collective-permute-done((bf16[128,1024]{1,0:T(8,128)(2,1)S(1)}, bf16[128,1024]{1,0:T(8,128)(2,1)S(1)}, u32[]{:S(2)}, u32[]{:S(2)}) %collective-permute-start.4) | collective-permute-done | bytes 262176 | tf_op jit(solution)/shard_map/ppermute | solution.py:294
  115.9 0.7 collective-permute-start.12
  116.6 0.0 collective-permute-done.2.rest_0_
  116.6 0.7 collective-permute-start.14
  117.3 0.0 collective-permute-done.6.rest_2_
  117.3 1.3 collective-permute-start.9
  118.6 0.0 collective-permute-done.10
  118.6 1.3 collective-permute-start.11
  119.9 0.0 collective-permute-done.12
  119.9 1.3 collective-permute-start.13
  121.2 0.0 collective-permute-done.14
  121.2 1.3 collective-permute-start.15
  122.5 14.5 %collective-permute-done.9.rest_4_ = bf16[32,1536]{1,0:T(8,128)(2,1)S(1)} collective-permute-done((bf16[32,1536]{1,0:T(8,128)(2,1)S(1)}, bf16[32,1536]{1,0:T(8,128)(2,1)S(1)}, u32[]{:S(2)}, u32[]{:S(2)}) %collective-permute-start.9) | collective-permute-done | bytes 98336 | tf_op jit(solution)/shard_map/ppermute | solution.py:294
  137.0 0.0 collective-permute-done.11.rest_5_
  137.0 0.0 collective-permute-done.13.rest_6_
  137.0 0.0 collective-permute-done.15.rest_7_
  137.0 0.0 collective-permute-done.near
  137.0 0.0 copy-start.2
  137.0 0.0 copy-start.3
  137.0 3.1 %mix.1 = bf16[512,1024]{1,0:T(8,128)(2,1)} custom-call(s32[1]{0:T(128)} %bitcast.4.first, bf16[512,1024]{1,0:T(8,128)(2,1)S(1)} %step.1.updated, bf16[512,1024]{1,0:T(8,128)(2,1)} %collective-permute-done.near, bf16[128,1024]{1,0:T(8,128)(2,1)S(1)} %collective-permute-done.2.rest_0_, bf16[128,1024]{1,0:T(8,128)(2,1)S(1)} %collective-permute-done.4.rest_1_, ...), custom_call_target="tpu_custom_call" | custom-call | tf_op jit(solution)/shard_map/mix/pallas_call | solution.py:262
  140.1 0.0 all-to-all-done.1.came_back
  140.1 1.1 combine.1
  (9 shorter events, 0.0 us)
Async XLA Ops:
  0.6 38.4 %copy-start = (bf16[1,1,512,1024]{3,2,1,0:T(8,128)(2,1)S(1)}, bf16[1,1,512,1024]{3,2,1,0:T(8,128)(2,1)}, u32[]{:S(2)}) copy-start(bf16[1,1,512,1024]{3,2,1,0:T(8,128)(2,1)} %param.11) | copy-start | bytes 3145732
  39.0 1.6 %copy-start.1 = (bf16[1,1024,1024]{2,1,0:T(8,128)(2,1)S(1)}, bf16[1,1024,1024]{2,1,0:T(8,128)(2,1)}, u32[]{:S(2)}) copy-start(bf16[1,1024,1024]{2,1,0:T(8,128)(2,1)} %param.10) | copy-start | bytes 6291460
  43.3 96.9 %all-to-all-start.1 = ((bf16[8,32,1024]{2,1,0:T(8,128)(2,1)}), bf16[8,32,1024]{2,1,0:T(8,128)(2,1)S(1)}, u32[]{:S(2)}, u32[]{:S(2)}) async-start(bf16[8,32,1024]{2,1,0:T(8,128)(2,1)} %get-tuple-element.15), calls=%async_computation.1 | async-start | bytes 1048576 | tf_op jit(solution)/shard_map/all_to_all | solution.py:308
  51.9 61.6 %copy-start.7 = (bf16[32,1536]{1,0:T(8,128)(2,1)S(1)}, bf16[32,1536]{1,0:T(8,128)(2,1)}, u32[]{:S(2)}) copy-start(bf16[32,1536]{1,0:T(8,128)(2,1)} %get-tuple-element.22) | copy-start | bytes 294916
  51.9 63.9 %copy-start.6 = (bf16[32,1536]{1,0:T(8,128)(2,1)S(1)}, bf16[32,1536]{1,0:T(8,128)(2,1)}, u32[]{:S(2)}) copy-start(bf16[32,1536]{1,0:T(8,128)(2,1)} %get-tuple-element.23) | copy-start | bytes 294916
  51.9 64.6 %copy-start.5 = (bf16[32,1536]{1,0:T(8,128)(2,1)S(1)}, bf16[32,1536]{1,0:T(8,128)(2,1)}, u32[]{:S(2)}) copy-start(bf16[32,1536]{1,0:T(8,128)(2,1)} %get-tuple-element.24) | copy-start | bytes 294916
  52.0 65.3 %copy-start.4 = (bf16[32,1536]{1,0:T(8,128)(2,1)S(1)}, bf16[32,1536]{1,0:T(8,128)(2,1)}, u32[]{:S(2)}) copy-start(bf16[32,1536]{1,0:T(8,128)(2,1)} %get-tuple-element.21) | copy-start | bytes 294916
  52.5 84.5 %collective-permute-start = (bf16[512,1024]{1,0:T(8,128)(2,1)S(1)}, bf16[512,1024]{1,0:T(8,128)(2,1)}, u32[]{:S(2)}, u32[]{:S(2)}) collective-permute-start(bf16[512,1024]{1,0:T(8,128)(2,1)S(1)} %step.1.updated), channel_id=1, source_target_pairs={{0,8},{8,16},{16,24},{24,32},{32,40},{40,48},{48,56},{56,64},{64,7... | collective-permute-start | bytes 3145736 | tf_op jit(solution)/shard_map/ppermute | solution.py:280
  54.8 2.7 %collective-permute-start.7 = (bf16[128,1024]{1,0:T(8,128)(2,1)S(1)}, bf16[128,1024]{1,0:T(8,128)(2,1)S(1)}, u32[]{:S(2)}, u32[]{:S(2)}) collective-permute-start(bf16[128,1024]{1,0:T(8,128)(2,1)S(1)} %get-tuple-element.25), channel_id=1, source_target_pairs={{248,96},{504,352},{760,608},{1016,864},{249,97},{505,353},{761,60... | collective-permute-start | bytes 786440 | tf_op jit(solution)/shard_map/ppermute | solution.py:290
  55.5 3.4 %collective-permute-start.3 = (bf16[128,1024]{1,0:T(8,128)(2,1)S(1)}, bf16[128,1024]{1,0:T(8,128)(2,1)S(1)}, u32[]{:S(2)}, u32[]{:S(2)}) collective-permute-start(bf16[128,1024]{1,0:T(8,128)(2,1)S(1)} %get-tuple-element.26), channel_id=1, source_target_pairs={{248,176},{504,432},{760,688},{1016,944},{249,177},{505,433},{761,... | collective-permute-start | bytes 786440 | tf_op jit(solution)/shard_map/ppermute | solution.py:290
  56.2 4.0 %collective-permute-start.1 = (bf16[128,1024]{1,0:T(8,128)(2,1)S(1)}, bf16[128,1024]{1,0:T(8,128)(2,1)S(1)}, u32[]{:S(2)}, u32[]{:S(2)}) collective-permute-start(bf16[128,1024]{1,0:T(8,128)(2,1)S(1)} %get-tuple-element.27), channel_id=1, source_target_pairs={{248,224},{504,480},{760,736},{1016,992},{249,225},{505,481},{761,... | collective-permute-start | bytes 786440 | tf_op jit(solution)/shard_map/ppermute | solution.py:290
  56.9 4.6 %collective-permute-start.5 = (bf16[128,1024]{1,0:T(8,128)(2,1)S(1)}, bf16[128,1024]{1,0:T(8,128)(2,1)S(1)}, u32[]{:S(2)}, u32[]{:S(2)}) collective-permute-start(bf16[128,1024]{1,0:T(8,128)(2,1)S(1)} %get-tuple-element.28), channel_id=1, source_target_pairs={{248,144},{504,400},{760,656},{1016,912},{249,145},{505,401},{761,... | collective-permute-start | bytes 786440 | tf_op jit(solution)/shard_map/ppermute | solution.py:290
  57.6 56.0 %collective-permute-start.8 = (bf16[128,1024]{1,0:T(8,128)(2,1)S(1)}, bf16[128,1024]{1,0:T(8,128)(2,1)S(1)}, u32[]{:S(2)}, u32[]{:S(2)}) collective-permute-start(bf16[128,1024]{1,0:T(8,128)(2,1)S(1)} %collective-permute-done.7), channel_id=1, source_target_pairs={{96,256},{352,512},{608,768},{864,0},{97,257},{353,513},{609,769},... | collective-permute-start | bytes 786440 | tf_op jit(solution)/shard_map/ppermute | solution.py:294
  58.9 57.0 %collective-permute-start.4 = (bf16[128,1024]{1,0:T(8,128)(2,1)S(1)}, bf16[128,1024]{1,0:T(8,128)(2,1)S(1)}, u32[]{:S(2)}, u32[]{:S(2)}) collective-permute-start(bf16[128,1024]{1,0:T(8,128)(2,1)S(1)} %collective-permute-done.3), channel_id=1, source_target_pairs={{176,256},{432,512},{688,768},{944,0},{177,257},{433,513},{689,769... | collective-permute-start | bytes 786440 | tf_op jit(solution)/shard_map/ppermute | solution.py:294
  60.2 56.4 %collective-permute-start.2 = (bf16[128,1024]{1,0:T(8,128)(2,1)S(1)}, bf16[128,1024]{1,0:T(8,128)(2,1)S(1)}, u32[]{:S(2)}, u32[]{:S(2)}) collective-permute-start(bf16[128,1024]{1,0:T(8,128)(2,1)S(1)} %collective-permute-done.1), channel_id=1, source_target_pairs={{224,256},{480,512},{736,768},{992,0},{225,257},{481,513},{737,769... | collective-permute-start | bytes 786440 | tf_op jit(solution)/shard_map/ppermute | solution.py:294
  61.5 55.7 %collective-permute-start.6 = (bf16[128,1024]{1,0:T(8,128)(2,1)S(1)}, bf16[128,1024]{1,0:T(8,128)(2,1)S(1)}, u32[]{:S(2)}, u32[]{:S(2)}) collective-permute-start(bf16[128,1024]{1,0:T(8,128)(2,1)S(1)} %collective-permute-done.5), channel_id=1, source_target_pairs={{144,256},{400,512},{656,768},{912,0},{145,257},{401,513},{657,769... | collective-permute-start | bytes 786440 | tf_op jit(solution)/shard_map/ppermute | solution.py:294
  113.6 5.0 %collective-permute-start.10 = (bf16[32,1536]{1,0:T(8,128)(2,1)S(1)}, bf16[32,1536]{1,0:T(8,128)(2,1)S(1)}, u32[]{:S(2)}, u32[]{:S(2)}) collective-permute-start(bf16[32,1536]{1,0:T(8,128)(2,1)S(1)} %copy-done.7), channel_id=1, source_target_pairs={{248,192},{504,448},{760,704},{1016,960},{249,193},{505,449},{761,... | collective-permute-start | bytes 294920 | tf_op jit(solution)/shard_map/ppermute | solution.py:290
  115.9 4.0 %collective-permute-start.12 = (bf16[32,1536]{1,0:T(8,128)(2,1)S(1)}, bf16[32,1536]{1,0:T(8,128)(2,1)S(1)}, u32[]{:S(2)}, u32[]{:S(2)}) collective-permute-start(bf16[32,1536]{1,0:T(8,128)(2,1)S(1)} %copy-done.6), channel_id=1, source_target_pairs={{248,56},{504,312},{760,568},{1016,824},{249,57},{505,313},{761,56... | collective-permute-start | bytes 294920 | tf_op jit(solution)/shard_map/ppermute | solution.py:290
  116.6 4.6 %collective-permute-start.14 = (bf16[32,1536]{1,0:T(8,128)(2,1)S(1)}, bf16[32,1536]{1,0:T(8,128)(2,1)S(1)}, u32[]{:S(2)}, u32[]{:S(2)}) collective-permute-start(bf16[32,1536]{1,0:T(8,128)(2,1)S(1)} %copy-done.5), channel_id=1, source_target_pairs={{248,8},{504,264},{760,520},{1016,776},{249,9},{505,265},{761,521}... | collective-permute-start | bytes 294920 | tf_op jit(solution)/shard_map/ppermute | solution.py:290
  117.3 19.7 %collective-permute-start.9 = (bf16[32,1536]{1,0:T(8,128)(2,1)S(1)}, bf16[32,1536]{1,0:T(8,128)(2,1)S(1)}, u32[]{:S(2)}, u32[]{:S(2)}) collective-permute-start(bf16[32,1536]{1,0:T(8,128)(2,1)S(1)} %copy-done.4), channel_id=1, source_target_pairs={{248,256},{504,512},{760,768},{1016,0},{249,257},{505,513},{761,76... | collective-permute-start | bytes 294920 | tf_op jit(solution)/shard_map/ppermute | solution.py:294
  118.6 18.4 %collective-permute-start.11 = (bf16[32,1536]{1,0:T(8,128)(2,1)S(1)}, bf16[32,1536]{1,0:T(8,128)(2,1)S(1)}, u32[]{:S(2)}, u32[]{:S(2)}) collective-permute-start(bf16[32,1536]{1,0:T(8,128)(2,1)S(1)} %collective-permute-done.10), channel_id=1, source_target_pairs={{192,256},{448,512},{704,768},{960,0},{193,257},{449,513},{705,769... | collective-permute-start | bytes 294920 | tf_op jit(solution)/shard_map/ppermute | solution.py:294
  119.9 17.1 %collective-permute-start.13 = (bf16[32,1536]{1,0:T(8,128)(2,1)S(1)}, bf16[32,1536]{1,0:T(8,128)(2,1)S(1)}, u32[]{:S(2)}, u32[]{:S(2)}) collective-permute-start(bf16[32,1536]{1,0:T(8,128)(2,1)S(1)} %collective-permute-done.12), channel_id=1, source_target_pairs={{56,256},{312,512},{568,768},{824,0},{57,257},{313,513},{569,769},... | collective-permute-start | bytes 294920 | tf_op jit(solution)/shard_map/ppermute | solution.py:294
  121.2 15.8 %collective-permute-start.15 = (bf16[32,1536]{1,0:T(8,128)(2,1)S(1)}, bf16[32,1536]{1,0:T(8,128)(2,1)S(1)}, u32[]{:S(2)}, u32[]{:S(2)}) collective-permute-start(bf16[32,1536]{1,0:T(8,128)(2,1)S(1)} %collective-permute-done.14), channel_id=1, source_target_pairs={{8,256},{264,512},{520,768},{776,0},{9,257},{265,513},{521,769},{7... | collective-permute-start | bytes 294920 | tf_op jit(solution)/shard_map/ppermute | solution.py:294
  137.0 3.1 %copy-start.2 = (f32[128,128]{1,0:T(8,128)S(1)}, f32[128,128]{1,0:T(8,128)}, u32[]{:S(2)}) copy-start(f32[128,128]{1,0:T(8,128)} %get-tuple-element.16.shares) | copy-start | bytes 196612
  137.0 3.1 %copy-start.3 = (bf16[128,128]{1,0:T(8,128)(2,1)S(1)}, bf16[128,128]{1,0:T(8,128)(2,1)}, u32[]{:S(2)}) copy-start(bf16[128,128]{1,0:T(8,128)(2,1)} %get-tuple-element.17.picks) | copy-start | bytes 98308

commit v3 on v2

--- a/solution.py
+++ b/solution.py
@@ -21,9 +21,28 @@
 
 
 LAST = place(3, 3, 1)
-EARLY_FROM = (place(3, 2, 0), place(2, 3, 0), place(2, 1, 0), place(1, 2, 0))
-LATE_FROM = (LAST, place(3, 0, 0), place(0, 3, 1), place(0, 0, 1))
+EARLY_FROM = (
+    place(1, 0, 0),
+    place(1, 3, 0),
+    place(1, 1, 0),
+    place(1, 2, 0),
+    place(0, 2, 0),
+    place(2, 0, 0),
+)
+EARLY_ROWS = (96, 96, 80, 80, 80, 80)
+LATE_FROM = (
+    place(3, 0, 0),
+    place(0, 3, 0),
+    place(0, 0, 1),
+    place(3, 2, 0),
+    place(2, 3, 0),
+    LAST,
+)
+LATE_ROWS = (32, 32, 16, 16, 16, 16)
+BEFORE_FROM = (place(3, 0, 0), LAST)
+BEFORE_ROWS = (48, 80)
 EARLY_PARTS = len(EARLY_FROM)
+BEFORE_PARTS = len(BEFORE_FROM)
 LATE_PARTS = len(LATE_FROM)
 
 
@@ -93,7 +112,7 @@
 
 
 def expert_kernel(arrived_in, project, weights, back_out, factors, *rest):
-    parts, (arrived, back, sems) = rest[:LATE_PARTS], rest[LATE_PARTS:]
+    parts, (arrived, back, sems) = rest[:-3], rest[-3:]
     sources, _, width = arrived.shape
     hidden_width = weights.shape[0]
     scale = hidden_width ** (-0.5)
@@ -106,14 +125,15 @@
     ]
     for load in loads:
         load.start()
-    height = rows[0] // len(parts)
     stores = [
         pltpu.make_async_copy(back.at[:, half], back_out.at[:, half], sems.at[2 + k])
         for k, half in enumerate(halves)
-    ] + [
-        pltpu.make_async_copy(factors.at[k * height : (k + 1) * height], part, sems.at[4 + k])
-        for k, part in enumerate(parts)
     ]
+    row = 0
+    for k, part in enumerate(parts):
+        height = part.shape[0]
+        stores.append(pltpu.make_async_copy(factors.at[row : row + height], part, sems.at[4 + k]))
+        row = (row + height) % rows[0]
     loads[0].wait()
     inputs = arrived[:, halves[0], :].reshape(rows)
     gate_pre = times(inputs, project[:, :hidden_width])
@@ -167,29 +187,39 @@
 
 def mix_kernel(first, updated, near, *rest):
     far_weights = rest[:EARLY_PARTS]
-    far_factors = rest[EARLY_PARTS : EARLY_PARTS + LATE_PARTS]
-    mixed, held_factors = rest[EARLY_PARTS + LATE_PARTS :]
-
-    def put(rows, neighbor):
-        mixed[rows, :] = (
-            (1.0 - mix_share) * updated[rows, :].astype(f32) + mix_share * neighbor.astype(f32)
+    far_after = rest[EARLY_PARTS : EARLY_PARTS + LATE_PARTS]
+    far_before = rest[EARLY_PARTS + LATE_PARTS : -3]
+    mixed, held_weights, held_factors = rest[-3:]
+
+    def put(neighbor):
+        mixed[...] = (
+            (1.0 - mix_share) * updated[...].astype(f32) + mix_share * neighbor.astype(f32)
         ).astype(bf16)
+
+    def hold(held, parts):
+        row = 0
+        for part in parts:
+            held[row : row + part.shape[0], :] = part[...]
+            row += part.shape[0]
 
     @pl.when(first[0] == 1)
     def _():
-        height = held_factors.shape[0] // LATE_PARTS
-        for k, part in enumerate(far_factors):
-            held_factors[k * height : (k + 1) * height, :] = part[...]
+        hold(held_factors, far_after)
+
+    @pl.when(first[0] == 2)
+    def _():
+        hold(held_factors, far_before)
+
+    @pl.when(first[0] != 0)
+    def _():
+        hold(held_weights, far_weights)
         hidden_width = updated.shape[0]
-        routed = held_factors[:, hidden_width:]
-        height = hidden_width // EARLY_PARTS
-        for k, part in enumerate(far_weights):
-            rows = slice(k * height, (k + 1) * height)
-            put(rows, stepped(part[...], held_factors[:, rows], routed, hidden_width))
-
-    @pl.when(first[0] != 1)
+        hidden, routed = held_factors[:, :hidden_width], held_factors[:, hidden_width:]
+        put(stepped(held_weights[...], hidden, routed, hidden_width))
+
+    @pl.when(first[0] == 0)
     def _():
-        put(slice(None), near[...])
+        put(near[...])
 
 
 def shape(dims, dtype=bf16):
@@ -227,13 +257,13 @@
     return pl.pallas_call(
         expert_kernel,
         out_shape=(pltpu.HBM(arrived.shape, bf16), shape((rows, columns)))
-        + (pltpu.HBM((rows // LATE_PARTS, columns), bf16),) * LATE_PARTS,
+        + tuple(pltpu.HBM((height, columns), bf16) for height in BEFORE_ROWS + LATE_ROWS),
         in_specs=[HBM, VMEM, VMEM],
-        out_specs=[HBM, VMEM] + [HBM] * LATE_PARTS,
+        out_specs=[HBM, VMEM] + [HBM] * (BEFORE_PARTS + LATE_PARTS),
         scratch_shapes=[
             pltpu.VMEM(arrived.shape, bf16),
             pltpu.VMEM(arrived.shape, bf16),
-            pltpu.SemaphoreType.DMA((4 + LATE_PARTS,)),
+            pltpu.SemaphoreType.DMA((4 + BEFORE_PARTS + LATE_PARTS,)),
         ],
         compiler_params=GRANT,
         name="expert_pass",
@@ -257,18 +287,23 @@
     )(weights, factors)
 
 
-def mix(first, updated, near, far_weights, far_factors):
-    rows, columns = far_factors[0].shape
+def mix(first, updated, near, far_weights, far_after, far_before):
+    rows = sum(LATE_ROWS)
+    columns = far_after[0].shape[1]
+    far = (*far_weights, *far_after, *far_before)
     return pl.pallas_call(
         mix_kernel,
         out_shape=shape(updated.shape),
         in_specs=[pl.BlockSpec(memory_space=pltpu.SMEM)]
-        + [VMEM] * (2 + len(far_weights) + len(far_factors)),
+        + [VMEM] * (2 + len(far)),
         out_specs=VMEM,
-        scratch_shapes=[pltpu.VMEM((rows * LATE_PARTS, columns), bf16)],
+        scratch_shapes=[
+            pltpu.VMEM(updated.shape, bf16),
+            pltpu.VMEM((rows, columns), bf16),
+        ],
         compiler_params=GRANT,
         name="mix",
-    )(first, updated, near, *far_weights, *far_factors)
+    )(first, updated, near, *far)
 
 
 def planes_of():
@@ -280,17 +315,17 @@
     return lax.ppermute(array, "replica", route)
 
 
-def to_next_plane(pieces, places):
+def to_next_plane(pieces, places, planes):
     held = []
     for piece, between in zip(pieces, places):
         if between == LAST:
             held.append(piece)
             continue
-        route = [(h + LAST, h + between) for h in planes_of()]
+        route = [(h + LAST, h + between) for h in planes]
         held.append(lax.ppermute(piece, "replica", route))
     far = []
     for piece, between in zip(held, places):
-        route = [(h + between, (h + PLANE) % lax.axis_size("replica")) for h in planes_of()]
+        route = [(h + between, (h + PLANE) % lax.axis_size("replica")) for h in planes]
         far.append(lax.ppermute(piece, "replica", route))
     return far
 
@@ -301,16 +336,22 @@
     project = gate_up[0]
     sent, shares, picks = pick(expert_ids.T, gate_weights.T, tokens, cotangent, experts)
     arrived = lax.all_to_all(sent, "expert", split_axis=0, concat_axis=0, tiled=True)
-    height = weights.shape[0] // EARLY_PARTS
-    pieces = [weights[k * height : (k + 1) * height] for k in range(EARLY_PARTS)]
-    far_weights = to_next_plane(pieces, EARLY_FROM)
+    pieces, row = [], 0
+    for height in EARLY_ROWS:
+        pieces.append(weights[row : row + height])
+        row += height
+    far_weights = to_next_plane(pieces, EARLY_FROM, planes_of())
     back, factors, *parts = expert_pass(arrived, project, weights)
     came_back = lax.all_to_all(back, "expert", split_axis=0, concat_axis=0, tiled=True)
     updated = step(weights, factors)
-    far_factors = to_next_plane(parts, LATE_FROM)
+    planes = planes_of()
+    far_before = to_next_plane(parts[:BEFORE_PARTS], BEFORE_FROM, planes[-1:])
+    far_after = to_next_plane(parts[BEFORE_PARTS:], LATE_FROM, planes[:-1])
     near = to_next(updated)
-    first = (lax.axis_index("replica") % PLANE == 0).astype(jnp.int32).reshape(1)
-    mixed = mix(first, updated, near, far_weights, far_factors)
+    place_index = lax.axis_index("replica")
+    first = jnp.where(place_index % PLANE == 0, jnp.where(place_index == 0, 2, 1), 0)
+    first = first.astype(jnp.int32).reshape(1)
+    mixed = mix(first, updated, near, far_weights, far_after, far_before)
     layer_out, token_grad = combine(came_back, shares, picks)
     return (layer_out, token_grad, mixed[None, None])
 

time: 142 us -> 185 us (1.30)
  the two profiles are of different devices: /device:TPU:96 before, /device:TPU:134 now
where the time goes in v3:
time: 185 us
  waiting for transfers between devices  71.1 us (38%)
  starting transfers between devices  67.4 us (36%)
  blocking collectives  34 us (18%)
  Pallas kernels  9.24 us (5%)
    ppermute x12, waiting for transfers between devices, to_next_plane(): held.append(lax.ppermute(piece, 'replica', route))  68.5 us
    ppermute x14, starting transfers between devices, to_next_plane(): far.append(lax.ppermute(piece, 'replica', route))  46 us
    all_to_all x1, blocking collectives, on_device(): lax.all_to_all(sent, 'expert', split_axis=0, concat_axis=0, tiled=True)  34 us
    all_to_all x1, starting transfers between devices, on_device(): lax.all_to_all(back, 'expert', split_axis=0, concat_axis=0, tiled=True)  10.3 us
    ppermute x12, starting transfers between devices, to_next_plane(): held.append(lax.ppermute(piece, 'replica', route))  9.28 us
  transfers between devices with their start and end apart: 28, of which 2 were waited for; matrix products, arithmetic and copies ran while one was open for 0% of the time, Pallas kernels for 2%

profile of v3, /device:TPU:134, one launch (start us, length us, event | category | flops | bytes accessed | tf_op | source)
XLA Modules:
  0.0 184.6 jit_solution(14515297281632178990)
XLA Ops:
  0.6 2.3 %pick.1 = (bf16[8,32,1024]{2,1,0:T(8,128)(2,1)}, f32[128,128]{1,0:T(8,128)}, bf16[128,128]{1,0:T(8,128)(2,1)}) custom-call(s32[8,128]{1,0:T(8,128)} %bitcast.22, f32[8,128]{1,0:T(8,128)} %bitcast.23, bf16[128,1024]{1,0:T(8,128)(2,1)} %tokens_in.1, bf16[128,1024]{1,0:T(8,128)(2,1)} %cotangent_in.1), custom_call_target="tpu_custom_call" | custom-call | tf_op jit(solution)/shard_map/pick/pallas_call | solution.py:242
  2.9 34.0 %all_to_all.10.arrived_in = bf16[8,32,1024]{2,1,0:T(8,128)(2,1)S(1)} all-to-all(bf16[8,32,1024]{2,1,0:T(8,128)(2,1)} %get-tuple-element.18), channel_id=1, replica_groups=mesh['replica'=128,'expert'=8] {'expert'}, dimensions={0} | all-to-all | bytes 1048576 | tf_op jit(solution)/shard_map/all_to_all | solution.py:338
  36.9 1.6 copy-done.1
  38.5 2.7 %expert_pass.1 = (bf16[8,32,1024]{2,1,0:T(8,128)(2,1)}, bf16[128,1536]{1,0:T(8,128)(2,1)S(1)}, bf16[48,1536]{1,0:T(8,128)(2,1)}, bf16[80,1536]{1,0:T(8,128)(2,1)...) custom-call(bf16[8,32,1024]{2,1,0:T(8,128)(2,1)S(1)} %all_to_all.10., ...), custom_call_target="tpu_custom_call" | custom-call | tf_op jit(solution)/shard_map/expert_pass/pallas_call | solution.py:257
  41.3 10.3 %all-to-all-start.1 = ((bf16[8,32,1024]{2,1,0:T(8,128)(2,1)}), bf16[8,32,1024]{2,1,0:T(8,128)(2,1)S(1)}, u32[]{:S(2)}, u32[]{:S(2)}) async-start(bf16[8,32,1024]{2,1,0:T(8,128)(2,1)} %get-tuple-element.19), calls=%async_computation.1 | async-start | bytes 1048576 | tf_op jit(solution)/shard_map/all_to_all | solution.py:345
  51.6 0.0 copy-start.4
  51.6 0.0 copy-start.6
  51.6 0.5 step.1.updated
  52.1 1.9 %collective-permute-start = (bf16[512,1024]{1,0:T(8,128)(2,1)S(1)}, bf16[512,1024]{1,0:T(8,128)(2,1)}, u32[]{:S(2)}, u32[]{:S(2)}) collective-permute-start(bf16[512,1024]{1,0:T(8,128)(2,1)S(1)} %step.1.updated), channel_id=1, source_target_pairs={{0,8},{8,16},{16,24},{24,32},{32,40},{40,48},{48,56},{56,64},{64,7... | collective-permute-start | bytes 3145736 | tf_op jit(solution)/shard_map/ppermute | solution.py:315
  54.1 0.7 collective-permute-start.11
  54.8 0.7 collective-permute-start.7
  55.4 0.7 collective-permute-start.5
  56.1 0.7 collective-permute-start.9
  56.9 0.7 collective-permute-start.3
  57.5 0.7 collective-permute-start.1
  58.2 0.0 collective-permute-done.5
  58.2 0.7 collective-permute-start.12
  58.9 0.0 collective-permute-done.9
  58.9 0.7 collective-permute-start.8
  59.6 0.7 collective-permute-start.6
  60.3 0.7 collective-permute-start.10
  61.0 0.0 collective-permute-done.12.rest_5_
  61.0 0.7 collective-permute-start.4
  61.7 0.0 collective-permute-done.8.rest_3_
  61.7 0.7 collective-permute-start.2
  62.4 0.0 collective-permute-done.6.rest_2_
  62.4 0.7 collective-permute-start.17
  63.1 0.0 collective-permute-done.10.rest_4_
  63.1 0.7 collective-permute-start.19
  63.8 0.7 collective-permute-start.21
  64.5 0.7 collective-permute-start.23
  65.1 0.0 collective-permute-done.17
  65.1 0.7 collective-permute-start.18
  65.8 0.0 collective-permute-done.19
  65.8 0.7 collective-permute-start.24
  66.5 0.0 collective-permute-done.21
  66.5 0.7 collective-permute-start.20
  67.2 0.7 collective-permute-start.22
  67.9 0.7 collective-permute-start.26
  68.6 1.3 collective-permute-start.13
  69.9 1.3 collective-permute-start.15
  71.2 0.7 collective-permute-start.25
  71.9 0.7 collective-permute-start.14
  72.6 68.5 %collective-permute-done.15 = bf16[32,1536]{1,0:T(8,128)(2,1)} collective-permute-done((bf16[32,1536]{1,0:T(8,128)(2,1)S(1)}, bf16[32,1536]{1,0:T(8,128)(2,1)}, u32[]{:S(2)}, u32[]{:S(2)}) %collective-permute-start.15) | collective-permute-done | bytes 98336 | tf_op jit(solution)/shard_map/ppermute | solution.py:325
  141.1 37.3 %collective-permute-start.16 = (bf16[32,1536]{1,0:T(8,128)(2,1)}, bf16[32,1536]{1,0:T(8,128)(2,1)S(1)}, u32[]{:S(2)}, u32[]{:S(2)}) collective-permute-start(bf16[32,1536]{1,0:T(8,128)(2,1)} %collective-permute-done.15), channel_id=1, source_target_pairs={{48,256},{304,512},{560,768},{49,257},{305,513},{561,769},{50,258}... | collective-permute-start | bytes 294920 | tf_op jit(solution)/shard_map/ppermute | solution.py:329
  178.4 2.5 %collective-permute-done.16.rest_7_ = bf16[32,1536]{1,0:T(8,128)(2,1)S(1)} collective-permute-done((bf16[32,1536]{1,0:T(8,128)(2,1)}, bf16[32,1536]{1,0:T(8,128)(2,1)S(1)}, u32[]{:S(2)}, u32[]{:S(2)}) %collective-permute-start.16) | collective-permute-done | bytes 98336 | tf_op jit(solution)/shard_map/ppermute | solution.py:329
  180.9 2.6 %mix.1 = bf16[512,1024]{1,0:T(8,128)(2,1)} custom-call(s32[1]{0:T(128)} %bitcast.4.first, bf16[512,1024]{1,0:T(8,128)(2,1)S(1)} %step.1.updated, bf16[512,1024]{1,0:T(8,128)(2,1)} %collective-permute-done.near, bf16[96,1024]{1,0:T(8,128)(2,1)S(1)} %collective-permute-done.2.rest_0_, bf16[96,1024]{1,0:T(8,128)(2,1)S(1)} %collective-permute-done.4.rest_1_, ...), custom_call_target="tpu_custom_call" | custom-call | tf_op jit(solution)/shard_map/mix/pallas_call | solution.py:294
  183.5 1.1 combine.1
  (38 shorter events, 0.2 us)
Async XLA Ops:
  0.6 36.3 %copy-start = (bf16[1,1,512,1024]{3,2,1,0:T(8,128)(2,1)S(1)}, bf16[1,1,512,1024]{3,2,1,0:T(8,128)(2,1)}, u32[]{:S(2)}) copy-start(bf16[1,1,512,1024]{3,2,1,0:T(8,128)(2,1)} %param.11) | copy-start | bytes 3145732
  36.9 1.6 copy-start.1
  41.3 142.2 %all-to-all-start.1 = ((bf16[8,32,1024]{2,1,0:T(8,128)(2,1)}), bf16[8,32,1024]{2,1,0:T(8,128)(2,1)S(1)}, u32[]{:S(2)}, u32[]{:S(2)}) async-start(bf16[8,32,1024]{2,1,0:T(8,128)(2,1)} %get-tuple-element.19), calls=%async_computation.1 | async-start | bytes 1048576 | tf_op jit(solution)/shard_map/all_to_all | solution.py:345
  51.5 10.8 %copy-start.10 = (bf16[16,1536]{1,0:T(8,128)(2,1)S(1)}, bf16[16,1536]{1,0:T(8,128)(2,1)}, u32[]{:S(2)}) copy-start(bf16[16,1536]{1,0:T(8,128)(2,1)} %get-tuple-element.27) | copy-start | bytes 147460
  51.6 11.5 %copy-start.9 = (bf16[16,1536]{1,0:T(8,128)(2,1)S(1)}, bf16[16,1536]{1,0:T(8,128)(2,1)}, u32[]{:S(2)}) copy-start(bf16[16,1536]{1,0:T(8,128)(2,1)} %get-tuple-element.28) | copy-start | bytes 147460
  51.6 12.2 %copy-start.8 = (bf16[16,1536]{1,0:T(8,128)(2,1)S(1)}, bf16[16,1536]{1,0:T(8,128)(2,1)}, u32[]{:S(2)}) copy-start(bf16[16,1536]{1,0:T(8,128)(2,1)} %get-tuple-element.29) | copy-start | bytes 147460
  51.6 12.9 %copy-start.7 = (bf16[16,1536]{1,0:T(8,128)(2,1)S(1)}, bf16[16,1536]{1,0:T(8,128)(2,1)}, u32[]{:S(2)}) copy-start(bf16[16,1536]{1,0:T(8,128)(2,1)} %get-tuple-element.30) | copy-start | bytes 147460
  51.6 14.3 %copy-start.4 = (bf16[48,1536]{1,0:T(8,128)(2,1)S(1)}, bf16[48,1536]{1,0:T(8,128)(2,1)}, u32[]{:S(2)}) copy-start(bf16[48,1536]{1,0:T(8,128)(2,1)} %get-tuple-element.31) | copy-start | bytes 442372
  51.6 17.0 %copy-start.6 = (bf16[32,1536]{1,0:T(8,128)(2,1)S(1)}, bf16[32,1536]{1,0:T(8,128)(2,1)}, u32[]{:S(2)}) copy-start(bf16[32,1536]{1,0:T(8,128)(2,1)} %get-tuple-element.25) | copy-start | bytes 294916
  51.6 18.3 %copy-start.5 = (bf16[32,1536]{1,0:T(8,128)(2,1)S(1)}, bf16[32,1536]{1,0:T(8,128)(2,1)}, u32[]{:S(2)}) copy-start(bf16[32,1536]{1,0:T(8,128)(2,1)} %get-tuple-element.26) | copy-start | bytes 294916
  52.1 128.7 %collective-permute-start = (bf16[512,1024]{1,0:T(8,128)(2,1)S(1)}, bf16[512,1024]{1,0:T(8,128)(2,1)}, u32[]{:S(2)}, u32[]{:S(2)}) collective-permute-start(bf16[512,1024]{1,0:T(8,128)(2,1)S(1)} %step.1.updated), channel_id=1, source_target_pairs={{0,8},{8,16},{16,24},{24,32},{32,40},{40,48},{48,56},{56,64},{64,7... | collective-permute-start | bytes 3145736 | tf_op jit(solution)/shard_map/ppermute | solution.py:315
  54.1 2.8 %collective-permute-start.11 = (bf16[80,1024]{1,0:T(8,128)(2,1)S(1)}, bf16[80,1024]{1,0:T(8,128)(2,1)S(1)}, u32[]{:S(2)}, u32[]{:S(2)}) collective-permute-start(bf16[80,1024]{1,0:T(8,128)(2,1)S(1)} %get-tuple-element.33), channel_id=1, source_target_pairs={{248,128},{504,384},{760,640},{1016,896},{249,129},{505,385},{761,... | collective-permute-start | bytes 491528 | tf_op jit(solution)/shard_map/ppermute | solution.py:325
  54.8 2.8 %collective-permute-start.7 = (bf16[80,1024]{1,0:T(8,128)(2,1)S(1)}, bf16[80,1024]{1,0:T(8,128)(2,1)S(1)}, u32[]{:S(2)}, u32[]{:S(2)}) collective-permute-start(bf16[80,1024]{1,0:T(8,128)(2,1)S(1)} %get-tuple-element.34), channel_id=1, source_target_pairs={{248,96},{504,352},{760,608},{1016,864},{249,97},{505,353},{761,60... | collective-permute-start | bytes 491528 | tf_op jit(solution)/shard_map/ppermute | solution.py:325
  55.4 2.8 %collective-permute-start.5 = (bf16[80,1024]{1,0:T(8,128)(2,1)S(1)}, bf16[80,1024]{1,0:T(8,128)(2,1)S(1)}, u32[]{:S(2)}, u32[]{:S(2)}) collective-permute-start(bf16[80,1024]{1,0:T(8,128)(2,1)S(1)} %get-tuple-element.35), channel_id=1, source_target_pairs={{248,80},{504,336},{760,592},{1016,848},{249,81},{505,337},{761,59... | collective-permute-start | bytes 491528 | tf_op jit(solution)/shard_map/ppermute | solution.py:325
  56.1 2.8 %collective-permute-start.9 = (bf16[80,1024]{1,0:T(8,128)(2,1)S(1)}, bf16[80,1024]{1,0:T(8,128)(2,1)S(1)}, u32[]{:S(2)}, u32[]{:S(2)}) collective-permute-start(bf16[80,1024]{1,0:T(8,128)(2,1)S(1)} %get-tuple-element.36), channel_id=1, source_target_pairs={{248,32},{504,288},{760,544},{1016,800},{249,33},{505,289},{761,54... | collective-permute-start | bytes 491528 | tf_op jit(solution)/shard_map/ppermute | solution.py:325
  56.9 2.8 %collective-permute-start.3 = (bf16[96,1024]{1,0:T(8,128)(2,1)S(1)}, bf16[96,1024]{1,0:T(8,128)(2,1)S(1)}, u32[]{:S(2)}, u32[]{:S(2)}) collective-permute-start(bf16[96,1024]{1,0:T(8,128)(2,1)S(1)} %get-tuple-element.37), channel_id=1, source_target_pairs={{248,112},{504,368},{760,624},{1016,880},{249,113},{505,369},{761,... | collective-permute-start | bytes 589832 | tf_op jit(solution)/shard_map/ppermute | solution.py:325
  57.5 2.8 %collective-permute-start.1 = (bf16[96,1024]{1,0:T(8,128)(2,1)S(1)}, bf16[96,1024]{1,0:T(8,128)(2,1)S(1)}, u32[]{:S(2)}, u32[]{:S(2)}) collective-permute-start(bf16[96,1024]{1,0:T(8,128)(2,1)S(1)} %get-tuple-element.38), channel_id=1, source_target_pairs={{248,64},{504,320},{760,576},{1016,832},{249,65},{505,321},{761,57... | collective-permute-start | bytes 589832 | tf_op jit(solution)/shard_map/ppermute | solution.py:325
  58.2 2.8 %collective-permute-start.12 = (bf16[80,1024]{1,0:T(8,128)(2,1)S(1)}, bf16[80,1024]{1,0:T(8,128)(2,1)S(1)}, u32[]{:S(2)}, u32[]{:S(2)}) collective-permute-start(bf16[80,1024]{1,0:T(8,128)(2,1)S(1)} %collective-permute-done.11), channel_id=1, source_target_pairs={{128,256},{384,512},{640,768},{896,0},{129,257},{385,513},{641,769... | collective-permute-start | bytes 491528 | tf_op jit(solution)/shard_map/ppermute | solution.py:329
  58.9 2.8 %collective-permute-start.8 = (bf16[80,1024]{1,0:T(8,128)(2,1)S(1)}, bf16[80,1024]{1,0:T(8,128)(2,1)S(1)}, u32[]{:S(2)}, u32[]{:S(2)}) collective-permute-start(bf16[80,1024]{1,0:T(8,128)(2,1)S(1)} %collective-permute-done.7), channel_id=1, source_target_pairs={{96,256},{352,512},{608,768},{864,0},{97,257},{353,513},{609,769},... | collective-permute-start | bytes 491528 | tf_op jit(solution)/shard_map/ppermute | solution.py:329
  59.6 2.8 %collective-permute-start.6 = (bf16[80,1024]{1,0:T(8,128)(2,1)S(1)}, bf16[80,1024]{1,0:T(8,128)(2,1)S(1)}, u32[]{:S(2)}, u32[]{:S(2)}) collective-permute-start(bf16[80,1024]{1,0:T(8,128)(2,1)S(1)} %collective-permute-done.5), channel_id=1, source_target_pairs={{80,256},{336,512},{592,768},{848,0},{81,257},{337,513},{593,769},... | collective-permute-start | bytes 491528 | tf_op jit(solution)/shard_map/ppermute | solution.py:329
  60.3 2.8 %collective-permute-start.10 = (bf16[80,1024]{1,0:T(8,128)(2,1)S(1)}, bf16[80,1024]{1,0:T(8,128)(2,1)S(1)}, u32[]{:S(2)}, u32[]{:S(2)}) collective-permute-start(bf16[80,1024]{1,0:T(8,128)(2,1)S(1)} %collective-permute-done.9), channel_id=1, source_target_pairs={{32,256},{288,512},{544,768},{800,0},{33,257},{289,513},{545,769},... | collective-permute-start | bytes 491528 | tf_op jit(solution)/shard_map/ppermute | solution.py:329
  61.0 2.8 %collective-permute-start.4 = (bf16[96,1024]{1,0:T(8,128)(2,1)S(1)}, bf16[96,1024]{1,0:T(8,128)(2,1)S(1)}, u32[]{:S(2)}, u32[]{:S(2)}) collective-permute-start(bf16[96,1024]{1,0:T(8,128)(2,1)S(1)} %collective-permute-done.3), channel_id=1, source_target_pairs={{112,256},{368,512},{624,768},{880,0},{113,257},{369,513},{625,769... | collective-permute-start | bytes 589832 | tf_op jit(solution)/shard_map/ppermute | solution.py:329
  61.7 2.8 %collective-permute-start.2 = (bf16[96,1024]{1,0:T(8,128)(2,1)S(1)}, bf16[96,1024]{1,0:T(8,128)(2,1)S(1)}, u32[]{:S(2)}, u32[]{:S(2)}) collective-permute-start(bf16[96,1024]{1,0:T(8,128)(2,1)S(1)} %collective-permute-done.1), channel_id=1, source_target_pairs={{64,256},{320,512},{576,768},{832,0},{65,257},{321,513},{577,769},... | collective-permute-start | bytes 589832 | tf_op jit(solution)/shard_map/ppermute | solution.py:329
  62.4 2.8 %collective-permute-start.17 = (bf16[16,1536]{1,0:T(8,128)(2,1)S(1)}, bf16[16,1536]{1,0:T(8,128)(2,1)S(1)}, u32[]{:S(2)}, u32[]{:S(2)}) collective-permute-start(bf16[16,1536]{1,0:T(8,128)(2,1)S(1)} %copy-done.10), channel_id=1, source_target_pairs={{248,8},{504,264},{760,520},{249,9},{505,265},{761,521},{250,10},{... | collective-permute-start | bytes 147464 | tf_op jit(solution)/shard_map/ppermute | solution.py:325
  63.1 2.7 %collective-permute-start.19 = (bf16[16,1536]{1,0:T(8,128)(2,1)S(1)}, bf16[16,1536]{1,0:T(8,128)(2,1)S(1)}, u32[]{:S(2)}, u32[]{:S(2)}) collective-permute-start(bf16[16,1536]{1,0:T(8,128)(2,1)S(1)} %copy-done.9), channel_id=1, source_target_pairs={{248,224},{504,480},{760,736},{249,225},{505,481},{761,737},{250,2... | collective-permute-start | bytes 147464 | tf_op jit(solution)/shard_map/ppermute | solution.py:325
  63.8 2.7 %collective-permute-start.21 = (bf16[16,1536]{1,0:T(8,128)(2,1)S(1)}, bf16[16,1536]{1,0:T(8,128)(2,1)S(1)}, u32[]{:S(2)}, u32[]{:S(2)}) collective-permute-start(bf16[16,1536]{1,0:T(8,128)(2,1)S(1)} %copy-done.8), channel_id=1, source_target_pairs={{248,176},{504,432},{760,688},{249,177},{505,433},{761,689},{250,1... | collective-permute-start | bytes 147464 | tf_op jit(solution)/shard_map/ppermute | solution.py:325
  64.5 2.7 %collective-permute-start.23 = (bf16[16,1536]{1,0:T(8,128)(2,1)S(1)}, bf16[16,1536]{1,0:T(8,128)(2,1)S(1)}, u32[]{:S(2)}, u32[]{:S(2)}) collective-permute-start(bf16[16,1536]{1,0:T(8,128)(2,1)S(1)} %copy-done.7), channel_id=1, source_target_pairs={{248,256},{504,512},{760,768},{249,257},{505,513},{761,769},{250,2... | collective-permute-start | bytes 147464 | tf_op jit(solution)/shard_map/ppermute | solution.py:329
  65.1 2.7 %collective-permute-start.18 = (bf16[16,1536]{1,0:T(8,128)(2,1)S(1)}, bf16[16,1536]{1,0:T(8,128)(2,1)S(1)}, u32[]{:S(2)}, u32[]{:S(2)}) collective-permute-start(bf16[16,1536]{1,0:T(8,128)(2,1)S(1)} %collective-permute-done.17), channel_id=1, source_target_pairs={{8,256},{264,512},{520,768},{9,257},{265,513},{521,769},{10,258},{... | collective-permute-start | bytes 147464 | tf_op jit(solution)/shard_map/ppermute | solution.py:329
  65.8 5.4 %collective-permute-start.24 = (bf16[48,1536]{1,0:T(8,128)(2,1)S(1)}, bf16[48,1536]{1,0:T(8,128)(2,1)S(1)}, u32[]{:S(2)}, u32[]{:S(2)}) collective-permute-start(bf16[48,1536]{1,0:T(8,128)(2,1)S(1)} %copy-done.4), channel_id=1, source_target_pairs={{1016,960},{1017,961},{1018,962},{1019,963},{1020,964},{1021,965},... | collective-permute-start | bytes 442376 | tf_op jit(solution)/shard_map/ppermute | solution.py:325
  66.5 2.1 %collective-permute-start.20 = (bf16[16,1536]{1,0:T(8,128)(2,1)S(1)}, bf16[16,1536]{1,0:T(8,128)(2,1)S(1)}, u32[]{:S(2)}, u32[]{:S(2)}) collective-permute-start(bf16[16,1536]{1,0:T(8,128)(2,1)S(1)} %collective-permute-done.19), channel_id=1, source_target_pairs={{224,256},{480,512},{736,768},{225,257},{481,513},{737,769},{226,2... | collective-permute-start | bytes 147464 | tf_op jit(solution)/shard_map/ppermute | solution.py:329
  67.2 2.7 %collective-permute-start.22 = (bf16[16,1536]{1,0:T(8,128)(2,1)S(1)}, bf16[16,1536]{1,0:T(8,128)(2,1)S(1)}, u32[]{:S(2)}, u32[]{:S(2)}) collective-permute-start(bf16[16,1536]{1,0:T(8,128)(2,1)S(1)} %collective-permute-done.21), channel_id=1, source_target_pairs={{176,256},{432,512},{688,768},{177,257},{433,513},{689,769},{178,2... | collective-permute-start | bytes 147464 | tf_op jit(solution)/shard_map/ppermute | solution.py:329
  67.9 113.0 %collective-permute-start.26 = (bf16[80,1536]{1,0:T(8,128)(2,1)}, bf16[80,1536]{1,0:T(8,128)(2,1)S(1)}, u32[]{:S(2)}, u32[]{:S(2)}) collective-permute-start(bf16[80,1536]{1,0:T(8,128)(2,1)} %get-tuple-element.32), channel_id=1, source_target_pairs={{1016,0},{1017,1},{1018,2},{1019,3},{1020,4},{1021,5},{1022,6},{10... | collective-permute-start | bytes 737288 | tf_op jit(solution)/shard_map/ppermute | solution.py:329
  68.6 3.3 %collective-permute-start.13 = (bf16[32,1536]{1,0:T(8,128)(2,1)S(1)}, bf16[32,1536]{1,0:T(8,128)(2,1)}, u32[]{:S(2)}, u32[]{:S(2)}) collective-permute-start(bf16[32,1536]{1,0:T(8,128)(2,1)S(1)} %copy-done.6), channel_id=1, source_target_pairs={{248,192},{504,448},{760,704},{249,193},{505,449},{761,705},{250,1... | collective-permute-start | bytes 294920 | tf_op jit(solution)/shard_map/ppermute | solution.py:325
  69.9 71.2 %collective-permute-start.15 = (bf16[32,1536]{1,0:T(8,128)(2,1)S(1)}, bf16[32,1536]{1,0:T(8,128)(2,1)}, u32[]{:S(2)}, u32[]{:S(2)}) collective-permute-start(bf16[32,1536]{1,0:T(8,128)(2,1)S(1)} %copy-done.5), channel_id=1, source_target_pairs={{248,48},{504,304},{760,560},{249,49},{505,305},{761,561},{250,50}... | collective-permute-start | bytes 294920 | tf_op jit(solution)/shard_map/ppermute | solution.py:325
  71.2 109.6 %collective-permute-start.25 = (bf16[48,1536]{1,0:T(8,128)(2,1)S(1)}, bf16[48,1536]{1,0:T(8,128)(2,1)S(1)}, u32[]{:S(2)}, u32[]{:S(2)}) collective-permute-start(bf16[48,1536]{1,0:T(8,128)(2,1)S(1)} %collective-permute-done.24), channel_id=1, source_target_pairs={{960,0},{961,1},{962,2},{963,3},{964,4},{965,5},{966,6},{967,7}} | collective-permute-start | bytes 442376 | tf_op jit(solution)/shard_map/ppermute | solution.py:329
  71.9 106.5 %collective-permute-start.14 = (bf16[32,1536]{1,0:T(8,128)(2,1)}, bf16[32,1536]{1,0:T(8,128)(2,1)S(1)}, u32[]{:S(2)}, u32[]{:S(2)}) collective-permute-start(bf16[32,1536]{1,0:T(8,128)(2,1)} %collective-permute-done.13), channel_id=1, source_target_pairs={{192,256},{448,512},{704,768},{193,257},{449,513},{705,769},{194,2... | collective-permute-start | bytes 294920 | tf_op jit(solution)/shard_map/ppermute | solution.py:329
  141.1 39.8 %collective-permute-start.16 = (bf16[32,1536]{1,0:T(8,128)(2,1)}, bf16[32,1536]{1,0:T(8,128)(2,1)S(1)}, u32[]{:S(2)}, u32[]{:S(2)}) collective-permute-start(bf16[32,1536]{1,0:T(8,128)(2,1)} %collective-permute-done.15), channel_id=1, source_target_pairs={{48,256},{304,512},{560,768},{49,257},{305,513},{561,769},{50,258}... | collective-permute-start | bytes 294920 | tf_op jit(solution)/shard_map/ppermute | solution.py:329
  180.9 2.6 %copy-start.2 = (f32[128,128]{1,0:T(8,128)S(1)}, f32[128,128]{1,0:T(8,128)}, u32[]{:S(2)}) copy-start(f32[128,128]{1,0:T(8,128)} %get-tuple-element.20.shares) | copy-start | bytes 196612
  180.9 2.6 %copy-start.3 = (bf16[128,128]{1,0:T(8,128)(2,1)S(1)}, bf16[128,128]{1,0:T(8,128)(2,1)}, u32[]{:S(2)}) copy-start(bf16[128,128]{1,0:T(8,128)(2,1)} %get-tuple-element.21.picks) | copy-start | bytes 98308

commit v4 on v3

--- a/solution.py
+++ b/solution.py
@@ -35,10 +35,9 @@
     place(0, 3, 0),
     place(0, 0, 1),
     place(3, 2, 0),
-    place(2, 3, 0),
     LAST,
 )
-LATE_ROWS = (32, 32, 16, 16, 16, 16)
+LATE_ROWS = (32, 32, 32, 16, 16)
 BEFORE_FROM = (place(3, 0, 0), LAST)
 BEFORE_ROWS = (48, 80)
 EARLY_PARTS = len(EARLY_FROM)
@@ -52,8 +51,8 @@
     )
 
 
-def pick_kernel(ids_in, gates_in, tokens_in, cotangent_in, sent_out, shares_out, picks_out, *own):
-    ids, gates, tokens, cotangent, sent, shares, picks, sems = own
+def pick_kernel(ids_in, gates_in, tokens_in, cotangent_in, sent_out, shares_out, *own):
+    ids, gates, tokens, cotangent, sent, shares, sems = own
     loads = [
         pltpu.make_async_copy(source, target, sems.at[k])
         for k, (source, target) in enumerate(
@@ -89,24 +88,21 @@
     share = jnp.where(picked, share, 0.0)
     shares[...] = share
     picked = picked.astype(bf16)
-    picks[...] = picked
     rows = (experts, CAP, width)
     first, second = slice(0, CAP), slice(CAP, 2 * CAP)
     stores = [
         pltpu.make_async_copy(shares, shares_out, sems.at[4]),
-        pltpu.make_async_copy(picks, picks_out, sems.at[5]),
-        pltpu.make_async_copy(sent.at[:, first], sent_out.at[:, first], sems.at[6]),
-        pltpu.make_async_copy(sent.at[:, second], sent_out.at[:, second], sems.at[7]),
+        pltpu.make_async_copy(sent.at[:, first], sent_out.at[:, first], sems.at[5]),
+        pltpu.make_async_copy(sent.at[:, second], sent_out.at[:, second], sems.at[6]),
     ]
     stores[0].start()
-    stores[1].start()
     loads[2].wait()
     sent[:, first, :] = times(picked, tokens[...]).astype(bf16).reshape(rows)
-    stores[2].start()
+    stores[1].start()
     slot_share = jnp.sum(share, axis=1, keepdims=True)
     loads[3].wait()
     sent[:, second, :] = (slot_share * times(picked, cotangent[...])).astype(bf16).reshape(rows)
-    stores[3].start()
+    stores[2].start()
     for store in stores:
         store.wait()
 
@@ -162,15 +158,16 @@
         store.wait()
 
 
-def combine_kernel(came_back, shares, picks, layer_out, token_grad):
+def combine_kernel(came_back, shares, layer_out, token_grad):
     experts = came_back.shape[0]
     rows = (experts * CAP, came_back.shape[2])
     share = shares[...]
+    picks = (share > 0.0).astype(bf16)
     upper = share.astype(bf16)
     lower = (share - upper.astype(f32)).astype(bf16)
     outputs = came_back[:, :CAP, :].reshape(rows)
     layer_out[...] = (times(upper, outputs, 0, 0) + times(lower, outputs, 0, 0)).astype(bf16)
-    token_grad[...] = times(picks[...], came_back[:, CAP:, :].reshape(rows), 0, 0).astype(bf16)
+    token_grad[...] = times(picks, came_back[:, CAP:, :].reshape(rows), 0, 0).astype(bf16)
 
 
 def stepped(weights, hidden, routed, hidden_width):
@@ -236,7 +233,6 @@
     outs = (
         shape((experts, 2 * CAP, width)),
         shape((experts * CAP, count), f32),
-        shape((experts * CAP, count)),
     )
     ins = (ids, gates, tokens, cotangent)
     return pl.pallas_call(
@@ -245,7 +241,7 @@
         in_specs=[HBM] * len(ins),
         out_specs=[HBM] * len(outs),
         scratch_shapes=[pltpu.VMEM(x.shape, x.dtype) for x in ins + outs]
-        + [pltpu.SemaphoreType.DMA((8,))],
+        + [pltpu.SemaphoreType.DMA((7,))],
         compiler_params=GRANT,
         name="pick",
     )(*(pltpu.with_memory_space_constraint(x, pltpu.HBM) for x in ins))
@@ -270,7 +266,7 @@
     )(arrived, project, weights)
 
 
-def combine(came_back, shares, picks):
+def combine(came_back, shares):
     count = shares.shape[1]
     width = came_back.shape[2]
     return pl.pallas_call(
@@ -278,7 +274,7 @@
         out_shape=(shape((count, width)), shape((count, width))),
         compiler_params=GRANT,
         name="combine",
-    )(came_back, shares, picks)
+    )(came_back, shares)
 
 
 def step(weights, factors):
@@ -334,7 +330,7 @@
     experts = lax.axis_size("expert")
     weights = down_weights[0, 0]
     project = gate_up[0]
-    sent, shares, picks = pick(expert_ids.T, gate_weights.T, tokens, cotangent, experts)
+    sent, shares = pick(expert_ids.T, gate_weights.T, tokens, cotangent, experts)
     arrived = lax.all_to_all(sent, "expert", split_axis=0, concat_axis=0, tiled=True)
     pieces, row = [], 0
     for height in EARLY_ROWS:
@@ -352,7 +348,7 @@
     first = jnp.where(place_index % PLANE == 0, jnp.where(place_index == 0, 2, 1), 0)
     first = first.astype(jnp.int32).reshape(1)
     mixed = mix(first, updated, near, far_weights, far_after, far_before)
-    layer_out, token_grad = combine(came_back, shares, picks)
+    layer_out, token_grad = combine(came_back, shares)
     return (layer_out, token_grad, mixed[None, None])
 
 

time: 185 us -> 178 us (0.962)
  the two profiles are of different devices: /device:TPU:134 before, /device:TPU:608 now
where the time goes in v4:
time: 178 us; the launch traced here: 177 us
  waiting for transfers between devices  98.1 us (55%)
  starting transfers between devices  35.1 us (20%)
  blocking collectives  31.2 us (18%)
  Pallas kernels  9.73 us (5%)
    ppermute x13, waiting for transfers between devices, to_next_plane(): far.append(lax.ppermute(piece, 'replica', route))  98.1 us
    all_to_all x1, blocking collectives, on_device(): lax.all_to_all(sent, 'expert', split_axis=0, concat_axis=0, tiled=True)  31.2 us
    ppermute x13, starting transfers between devices, to_next_plane(): far.append(lax.ppermute(piece, 'replica', route))  15.5 us
    all_to_all x1, starting transfers between devices, on_device(): lax.all_to_all(back, 'expert', split_axis=0, concat_axis=0, tiled=True)  8.69 us
    ppermute x11, starting transfers between devices, to_next_plane(): held.append(lax.ppermute(piece, 'replica', route))  8.62 us
  transfers between devices with their start and end apart: 26, of which 7 were waited for; matrix products, arithmetic and copies ran while one was open for 0% of the time, Pallas kernels for 2%

profile of v4, /device:TPU:608, one launch (start us, length us, event | category | flops | bytes accessed | tf_op | source)
XLA Modules:
  0.0 176.9 jit_solution(5859070376160536266)
XLA Ops:
  0.6 2.3 %pick.1 = (bf16[8,32,1024]{2,1,0:T(8,128)(2,1)}, f32[128,128]{1,0:T(8,128)}) custom-call(s32[8,128]{1,0:T(8,128)} %bitcast.22, f32[8,128]{1,0:T(8,128)} %bitcast.23, bf16[128,1024]{1,0:T(8,128)(2,1)} %tokens_in.1, bf16[128,1024]{1,0:T(8,128)(2,1)} %cotangent_in.1), custom_call_target="tpu_custom_call" | custom-call | tf_op jit(solution)/shard_map/pick/pallas_call | solution.py:238
  2.9 31.2 %all_to_all.10.arrived_in = bf16[8,32,1024]{2,1,0:T(8,128)(2,1)S(1)} all-to-all(bf16[8,32,1024]{2,1,0:T(8,128)(2,1)} %get-tuple-element.16), channel_id=1, replica_groups=mesh['replica'=128,'expert'=8] {'expert'}, dimensions={0} | all-to-all | bytes 1048576 | tf_op jit(solution)/shard_map/all_to_all | solution.py:334
  34.2 1.6 copy-done.1
  35.8 2.7 %expert_pass.1 = (bf16[8,32,1024]{2,1,0:T(8,128)(2,1)}, bf16[128,1536]{1,0:T(8,128)(2,1)S(1)}, bf16[48,1536]{1,0:T(8,128)(2,1)}, bf16[80,1536]{1,0:T(8,128)(2,1)...) custom-call(bf16[8,32,1024]{2,1,0:T(8,128)(2,1)S(1)} %all_to_all.10., ...), custom_call_target="tpu_custom_call" | custom-call | tf_op jit(solution)/shard_map/expert_pass/pallas_call | solution.py:253
  38.5 8.7 %all-to-all-start.1 = ((bf16[8,32,1024]{2,1,0:T(8,128)(2,1)}), bf16[8,32,1024]{2,1,0:T(8,128)(2,1)S(1)}, u32[]{:S(2)}, u32[]{:S(2)}) async-start(bf16[8,32,1024]{2,1,0:T(8,128)(2,1)} %get-tuple-element.17), calls=%async_computation.1 | async-start | bytes 1048576 | tf_op jit(solution)/shard_map/all_to_all | solution.py:341
  47.2 0.0 copy-start.3
  47.2 0.5 step.1.updated
  47.7 2.3 %collective-permute-start = (bf16[512,1024]{1,0:T(8,128)(2,1)S(1)}, bf16[512,1024]{1,0:T(8,128)(2,1)}, u32[]{:S(2)}, u32[]{:S(2)}) collective-permute-start(bf16[512,1024]{1,0:T(8,128)(2,1)S(1)} %step.1.updated), channel_id=1, source_target_pairs={{0,8},{8,16},{16,24},{24,32},{32,40},{40,48},{48,56},{56,64},{64,7... | collective-permute-start | bytes 3145736 | tf_op jit(solution)/shard_map/ppermute | solution.py:311
  50.0 0.7 collective-permute-start.11
  50.7 0.7 collective-permute-start.7
  51.4 0.7 collective-permute-start.5
  52.1 0.7 collective-permute-start.9
  52.8 0.0 collective-permute-done.11
  52.8 0.7 collective-permute-start.3
  53.5 0.0 collective-permute-done.7
  53.5 0.7 collective-permute-start.1
  54.2 0.0 collective-permute-done.5
  54.2 1.3 collective-permute-start.12
  55.5 0.0 collective-permute-done.9
  55.5 1.3 collective-permute-start.8
  56.8 1.3 collective-permute-start.6
  58.1 0.0 collective-permute-done.1
  58.1 1.3 collective-permute-start.10
  59.4 31.1 %collective-permute-done.12.rest_5_ = bf16[80,1024]{1,0:T(8,128)(2,1)S(1)} collective-permute-done((bf16[80,1024]{1,0:T(8,128)(2,1)S(1)}, bf16[80,1024]{1,0:T(8,128)(2,1)S(1)}, u32[]{:S(2)}, u32[]{:S(2)}) %collective-permute-start.12) | collective-permute-done | bytes 163872 | tf_op jit(solution)/shard_map/ppermute | solution.py:325
  90.5 1.3 collective-permute-start.4
  91.8 0.0 collective-permute-done.8.rest_3_
  91.8 1.3 collective-permute-start.2
  93.1 0.0 collective-permute-done.6.rest_2_
  93.1 0.7 collective-permute-start.19
  93.8 1.3 collective-permute-start.21
  95.1 21.5 %collective-permute-done.4.rest_1_ = bf16[96,1024]{1,0:T(8,128)(2,1)S(1)} collective-permute-done((bf16[96,1024]{1,0:T(8,128)(2,1)S(1)}, bf16[96,1024]{1,0:T(8,128)(2,1)S(1)}, u32[]{:S(2)}, u32[]{:S(2)}) %collective-permute-start.4) | collective-permute-done | bytes 196640 | tf_op jit(solution)/shard_map/ppermute | solution.py:325
  116.6 0.7 collective-permute-start.13
  117.3 0.7 collective-permute-done.2.rest_0_
  118.0 1.3 collective-permute-start.15
  119.3 1.3 collective-permute-start.20
  120.6 0.7 collective-permute-start.22
  121.3 17.2 %collective-permute-done.20.rest_9_ = bf16[16,1536]{1,0:T(8,128)(2,1)S(1)} collective-permute-done((bf16[16,1536]{1,0:T(8,128)(2,1)S(1)}, bf16[16,1536]{1,0:T(8,128)(2,1)S(1)}, u32[]{:S(2)}, u32[]{:S(2)}) %collective-permute-start.20) | collective-permute-done | bytes 49184 | tf_op jit(solution)/shard_map/ppermute | solution.py:325
  138.5 0.7 collective-permute-start.24
  139.2 1.3 collective-permute-start.17
  140.5 1.3 collective-permute-start.14
  141.8 0.7 collective-permute-start.23
  142.5 1.3 collective-permute-start.16
  143.8 14.0 %collective-permute-done.14.rest_6_ = bf16[32,1536]{1,0:T(8,128)(2,1)S(1)} collective-permute-done((bf16[32,1536]{1,0:T(8,128)(2,1)S(1)}, bf16[32,1536]{1,0:T(8,128)(2,1)S(1)}, u32[]{:S(2)}, u32[]{:S(2)}) %collective-permute-start.14) | collective-permute-done | bytes 98336 | tf_op jit(solution)/shard_map/ppermute | solution.py:325
  157.8 1.3 collective-permute-start.18
  159.1 0.9 collective-permute-done.16.rest_7_
  160.0 12.6 %collective-permute-done.18.rest_8_ = bf16[32,1536]{1,0:T(8,128)(2,1)S(1)} collective-permute-done((bf16[32,1536]{1,0:T(8,128)(2,1)}, bf16[32,1536]{1,0:T(8,128)(2,1)S(1)}, u32[]{:S(2)}, u32[]{:S(2)}) %collective-permute-start.18) | collective-permute-done | bytes 98336 | tf_op jit(solution)/shard_map/ppermute | solution.py:325
  172.7 3.1 %mix.1 = bf16[512,1024]{1,0:T(8,128)(2,1)} custom-call(s32[1]{0:T(128)} %bitcast.4.first, bf16[512,1024]{1,0:T(8,128)(2,1)S(1)} %step.1.updated, bf16[512,1024]{1,0:T(8,128)(2,1)} %collective-permute-done.near, bf16[96,1024]{1,0:T(8,128)(2,1)S(1)} %collective-permute-done.2.rest_0_, bf16[96,1024]{1,0:T(8,128)(2,1)S(1)} %collective-permute-done.4.rest_1_, ...), custom_call_target="tpu_custom_call" | custom-call | tf_op jit(solution)/shard_map/mix/pallas_call | solution.py:290
  175.8 1.1 combine.1
  (30 shorter events, 0.1 us)
Async XLA Ops:
  0.6 33.5 %copy-start = (bf16[1,1,512,1024]{3,2,1,0:T(8,128)(2,1)S(1)}, bf16[1,1,512,1024]{3,2,1,0:T(8,128)(2,1)}, u32[]{:S(2)}) copy-start(bf16[1,1,512,1024]{3,2,1,0:T(8,128)(2,1)} %param.11) | copy-start | bytes 3145732
  34.2 1.6 copy-start.1
  38.5 137.3 %all-to-all-start.1 = ((bf16[8,32,1024]{2,1,0:T(8,128)(2,1)}), bf16[8,32,1024]{2,1,0:T(8,128)(2,1)S(1)}, u32[]{:S(2)}, u32[]{:S(2)}) async-start(bf16[8,32,1024]{2,1,0:T(8,128)(2,1)} %get-tuple-element.17), calls=%async_computation.1 | async-start | bytes 1048576 | tf_op jit(solution)/shard_map/all_to_all | solution.py:341
  47.2 45.9 %copy-start.8 = (bf16[16,1536]{1,0:T(8,128)(2,1)S(1)}, bf16[16,1536]{1,0:T(8,128)(2,1)}, u32[]{:S(2)}) copy-start(bf16[16,1536]{1,0:T(8,128)(2,1)} %get-tuple-element.25) | copy-start | bytes 147460
  47.2 46.6 %copy-start.7 = (bf16[16,1536]{1,0:T(8,128)(2,1)S(1)}, bf16[16,1536]{1,0:T(8,128)(2,1)}, u32[]{:S(2)}) copy-start(bf16[16,1536]{1,0:T(8,128)(2,1)} %get-tuple-element.26) | copy-start | bytes 147460
  47.2 69.4 %copy-start.6 = (bf16[32,1536]{1,0:T(8,128)(2,1)S(1)}, bf16[32,1536]{1,0:T(8,128)(2,1)}, u32[]{:S(2)}) copy-start(bf16[32,1536]{1,0:T(8,128)(2,1)} %get-tuple-element.22) | copy-start | bytes 294916
  47.2 70.8 %copy-start.5 = (bf16[32,1536]{1,0:T(8,128)(2,1)S(1)}, bf16[32,1536]{1,0:T(8,128)(2,1)}, u32[]{:S(2)}) copy-start(bf16[32,1536]{1,0:T(8,128)(2,1)} %get-tuple-element.23) | copy-start | bytes 294916
  47.2 73.4 %copy-start.3 = (bf16[48,1536]{1,0:T(8,128)(2,1)S(1)}, bf16[48,1536]{1,0:T(8,128)(2,1)}, u32[]{:S(2)}) copy-start(bf16[48,1536]{1,0:T(8,128)(2,1)} %get-tuple-element.27) | copy-start | bytes 442372
  47.2 92.0 %copy-start.4 = (bf16[32,1536]{1,0:T(8,128)(2,1)S(1)}, bf16[32,1536]{1,0:T(8,128)(2,1)}, u32[]{:S(2)}) copy-start(bf16[32,1536]{1,0:T(8,128)(2,1)} %get-tuple-element.24) | copy-start | bytes 294916
  47.7 125.0 %collective-permute-start = (bf16[512,1024]{1,0:T(8,128)(2,1)S(1)}, bf16[512,1024]{1,0:T(8,128)(2,1)}, u32[]{:S(2)}, u32[]{:S(2)}) collective-permute-start(bf16[512,1024]{1,0:T(8,128)(2,1)S(1)} %step.1.updated), channel_id=1, source_target_pairs={{0,8},{8,16},{16,24},{24,32},{32,40},{40,48},{48,56},{56,64},{64,7... | collective-permute-start | bytes 3145736 | tf_op jit(solution)/shard_map/ppermute | solution.py:311
  50.0 2.8 %collective-permute-start.11 = (bf16[80,1024]{1,0:T(8,128)(2,1)S(1)}, bf16[80,1024]{1,0:T(8,128)(2,1)S(1)}, u32[]{:S(2)}, u32[]{:S(2)}) collective-permute-start(bf16[80,1024]{1,0:T(8,128)(2,1)S(1)} %get-tuple-element.29), channel_id=1, source_target_pairs={{248,128},{504,384},{760,640},{1016,896},{249,129},{505,385},{761,... | collective-permute-start | bytes 491528 | tf_op jit(solution)/shard_map/ppermute | solution.py:321
  50.7 2.8 %collective-permute-start.7 = (bf16[80,1024]{1,0:T(8,128)(2,1)S(1)}, bf16[80,1024]{1,0:T(8,128)(2,1)S(1)}, u32[]{:S(2)}, u32[]{:S(2)}) collective-permute-start(bf16[80,1024]{1,0:T(8,128)(2,1)S(1)} %get-tuple-element.30), channel_id=1, source_target_pairs={{248,96},{504,352},{760,608},{1016,864},{249,97},{505,353},{761,60... | collective-permute-start | bytes 491528 | tf_op jit(solution)/shard_map/ppermute | solution.py:321
  51.4 2.8 %collective-permute-start.5 = (bf16[80,1024]{1,0:T(8,128)(2,1)S(1)}, bf16[80,1024]{1,0:T(8,128)(2,1)S(1)}, u32[]{:S(2)}, u32[]{:S(2)}) collective-permute-start(bf16[80,1024]{1,0:T(8,128)(2,1)S(1)} %get-tuple-element.31), channel_id=1, source_target_pairs={{248,80},{504,336},{760,592},{1016,848},{249,81},{505,337},{761,59... | collective-permute-start | bytes 491528 | tf_op jit(solution)/shard_map/ppermute | solution.py:321
  52.1 3.4 %collective-permute-start.9 = (bf16[80,1024]{1,0:T(8,128)(2,1)S(1)}, bf16[80,1024]{1,0:T(8,128)(2,1)S(1)}, u32[]{:S(2)}, u32[]{:S(2)}) collective-permute-start(bf16[80,1024]{1,0:T(8,128)(2,1)S(1)} %get-tuple-element.32), channel_id=1, source_target_pairs={{248,32},{504,288},{760,544},{1016,800},{249,33},{505,289},{761,54... | collective-permute-start | bytes 491528 | tf_op jit(solution)/shard_map/ppermute | solution.py:321
  52.8 4.0 %collective-permute-start.3 = (bf16[96,1024]{1,0:T(8,128)(2,1)S(1)}, bf16[96,1024]{1,0:T(8,128)(2,1)S(1)}, u32[]{:S(2)}, u32[]{:S(2)}) collective-permute-start(bf16[96,1024]{1,0:T(8,128)(2,1)S(1)} %get-tuple-element.33), channel_id=1, source_target_pairs={{248,112},{504,368},{760,624},{1016,880},{249,113},{505,369},{761,... | collective-permute-start | bytes 589832 | tf_op jit(solution)/shard_map/ppermute | solution.py:321
  53.5 4.6 %collective-permute-start.1 = (bf16[96,1024]{1,0:T(8,128)(2,1)S(1)}, bf16[96,1024]{1,0:T(8,128)(2,1)S(1)}, u32[]{:S(2)}, u32[]{:S(2)}) collective-permute-start(bf16[96,1024]{1,0:T(8,128)(2,1)S(1)} %get-tuple-element.34), channel_id=1, source_target_pairs={{248,64},{504,320},{760,576},{1016,832},{249,65},{505,321},{761,57... | collective-permute-start | bytes 589832 | tf_op jit(solution)/shard_map/ppermute | solution.py:321
  54.2 36.3 %collective-permute-start.12 = (bf16[80,1024]{1,0:T(8,128)(2,1)S(1)}, bf16[80,1024]{1,0:T(8,128)(2,1)S(1)}, u32[]{:S(2)}, u32[]{:S(2)}) collective-permute-start(bf16[80,1024]{1,0:T(8,128)(2,1)S(1)} %collective-permute-done.11), channel_id=1, source_target_pairs={{128,256},{384,512},{640,768},{896,0},{129,257},{385,513},{641,769... | collective-permute-start | bytes 491528 | tf_op jit(solution)/shard_map/ppermute | solution.py:325
  55.5 36.3 %collective-permute-start.8 = (bf16[80,1024]{1,0:T(8,128)(2,1)S(1)}, bf16[80,1024]{1,0:T(8,128)(2,1)S(1)}, u32[]{:S(2)}, u32[]{:S(2)}) collective-permute-start(bf16[80,1024]{1,0:T(8,128)(2,1)S(1)} %collective-permute-done.7), channel_id=1, source_target_pairs={{96,256},{352,512},{608,768},{864,0},{97,257},{353,513},{609,769},... | collective-permute-start | bytes 491528 | tf_op jit(solution)/shard_map/ppermute | solution.py:325
  56.8 36.3 %collective-permute-start.6 = (bf16[80,1024]{1,0:T(8,128)(2,1)S(1)}, bf16[80,1024]{1,0:T(8,128)(2,1)S(1)}, u32[]{:S(2)}, u32[]{:S(2)}) collective-permute-start(bf16[80,1024]{1,0:T(8,128)(2,1)S(1)} %collective-permute-done.5), channel_id=1, source_target_pairs={{80,256},{336,512},{592,768},{848,0},{81,257},{337,513},{593,769},... | collective-permute-start | bytes 491528 | tf_op jit(solution)/shard_map/ppermute | solution.py:325
  58.1 35.7 %collective-permute-start.10 = (bf16[80,1024]{1,0:T(8,128)(2,1)S(1)}, bf16[80,1024]{1,0:T(8,128)(2,1)S(1)}, u32[]{:S(2)}, u32[]{:S(2)}) collective-permute-start(bf16[80,1024]{1,0:T(8,128)(2,1)S(1)} %collective-permute-done.9), channel_id=1, source_target_pairs={{32,256},{288,512},{544,768},{800,0},{33,257},{289,513},{545,769},... | collective-permute-start | bytes 491528 | tf_op jit(solution)/shard_map/ppermute | solution.py:325
  90.5 26.1 %collective-permute-start.4 = (bf16[96,1024]{1,0:T(8,128)(2,1)S(1)}, bf16[96,1024]{1,0:T(8,128)(2,1)S(1)}, u32[]{:S(2)}, u32[]{:S(2)}) collective-permute-start(bf16[96,1024]{1,0:T(8,128)(2,1)S(1)} %collective-permute-done.3), channel_id=1, source_target_pairs={{112,256},{368,512},{624,768},{880,0},{113,257},{369,513},{625,769... | collective-permute-start | bytes 589832 | tf_op jit(solution)/shard_map/ppermute | solution.py:325
  91.8 26.2 %collective-permute-start.2 = (bf16[96,1024]{1,0:T(8,128)(2,1)S(1)}, bf16[96,1024]{1,0:T(8,128)(2,1)S(1)}, u32[]{:S(2)}, u32[]{:S(2)}) collective-permute-start(bf16[96,1024]{1,0:T(8,128)(2,1)S(1)} %collective-permute-done.1), channel_id=1, source_target_pairs={{64,256},{320,512},{576,768},{832,0},{65,257},{321,513},{577,769},... | collective-permute-start | bytes 589832 | tf_op jit(solution)/shard_map/ppermute | solution.py:325
  93.1 26.2 %collective-permute-start.19 = (bf16[16,1536]{1,0:T(8,128)(2,1)S(1)}, bf16[16,1536]{1,0:T(8,128)(2,1)S(1)}, u32[]{:S(2)}, u32[]{:S(2)}) collective-permute-start(bf16[16,1536]{1,0:T(8,128)(2,1)S(1)} %copy-done.8), channel_id=1, source_target_pairs={{248,224},{504,480},{760,736},{249,225},{505,481},{761,737},{250,2... | collective-permute-start | bytes 147464 | tf_op jit(solution)/shard_map/ppermute | solution.py:321
  93.8 26.8 %collective-permute-start.21 = (bf16[16,1536]{1,0:T(8,128)(2,1)S(1)}, bf16[16,1536]{1,0:T(8,128)(2,1)S(1)}, u32[]{:S(2)}, u32[]{:S(2)}) collective-permute-start(bf16[16,1536]{1,0:T(8,128)(2,1)S(1)} %copy-done.7), channel_id=1, source_target_pairs={{248,256},{504,512},{760,768},{249,257},{505,513},{761,769},{250,2... | collective-permute-start | bytes 147464 | tf_op jit(solution)/shard_map/ppermute | solution.py:325
  116.6 22.6 %collective-permute-start.13 = (bf16[32,1536]{1,0:T(8,128)(2,1)S(1)}, bf16[32,1536]{1,0:T(8,128)(2,1)S(1)}, u32[]{:S(2)}, u32[]{:S(2)}) collective-permute-start(bf16[32,1536]{1,0:T(8,128)(2,1)S(1)} %copy-done.6), channel_id=1, source_target_pairs={{248,192},{504,448},{760,704},{249,193},{505,449},{761,705},{250,1... | collective-permute-start | bytes 294920 | tf_op jit(solution)/shard_map/ppermute | solution.py:321
  118.0 22.5 %collective-permute-start.15 = (bf16[32,1536]{1,0:T(8,128)(2,1)S(1)}, bf16[32,1536]{1,0:T(8,128)(2,1)}, u32[]{:S(2)}, u32[]{:S(2)}) collective-permute-start(bf16[32,1536]{1,0:T(8,128)(2,1)S(1)} %copy-done.5), channel_id=1, source_target_pairs={{248,48},{504,304},{760,560},{249,49},{505,305},{761,561},{250,50}... | collective-permute-start | bytes 294920 | tf_op jit(solution)/shard_map/ppermute | solution.py:321
  119.3 19.2 %collective-permute-start.20 = (bf16[16,1536]{1,0:T(8,128)(2,1)S(1)}, bf16[16,1536]{1,0:T(8,128)(2,1)S(1)}, u32[]{:S(2)}, u32[]{:S(2)}) collective-permute-start(bf16[16,1536]{1,0:T(8,128)(2,1)S(1)} %collective-permute-done.19), channel_id=1, source_target_pairs={{224,256},{480,512},{736,768},{225,257},{481,513},{737,769},{226,2... | collective-permute-start | bytes 147464 | tf_op jit(solution)/shard_map/ppermute | solution.py:325
  120.6 21.2 %collective-permute-start.22 = (bf16[48,1536]{1,0:T(8,128)(2,1)S(1)}, bf16[48,1536]{1,0:T(8,128)(2,1)S(1)}, u32[]{:S(2)}, u32[]{:S(2)}) collective-permute-start(bf16[48,1536]{1,0:T(8,128)(2,1)S(1)} %copy-done.3), channel_id=1, source_target_pairs={{1016,960},{1017,961},{1018,962},{1019,963},{1020,964},{1021,965},... | collective-permute-start | bytes 442376 | tf_op jit(solution)/shard_map/ppermute | solution.py:321
  138.5 34.2 %collective-permute-start.24 = (bf16[80,1536]{1,0:T(8,128)(2,1)}, bf16[80,1536]{1,0:T(8,128)(2,1)S(1)}, u32[]{:S(2)}, u32[]{:S(2)}) collective-permute-start(bf16[80,1536]{1,0:T(8,128)(2,1)} %get-tuple-element.28), channel_id=1, source_target_pairs={{1016,0},{1017,1},{1018,2},{1019,3},{1020,4},{1021,5},{1022,6},{10... | collective-permute-start | bytes 737288 | tf_op jit(solution)/shard_map/ppermute | solution.py:325
  139.2 3.3 %collective-permute-start.17 = (bf16[32,1536]{1,0:T(8,128)(2,1)S(1)}, bf16[32,1536]{1,0:T(8,128)(2,1)}, u32[]{:S(2)}, u32[]{:S(2)}) collective-permute-start(bf16[32,1536]{1,0:T(8,128)(2,1)S(1)} %copy-done.4), channel_id=1, source_target_pairs={{248,8},{504,264},{760,520},{249,9},{505,265},{761,521},{250,10},{... | collective-permute-start | bytes 294920 | tf_op jit(solution)/shard_map/ppermute | solution.py:321
  140.5 17.3 %collective-permute-start.14 = (bf16[32,1536]{1,0:T(8,128)(2,1)S(1)}, bf16[32,1536]{1,0:T(8,128)(2,1)S(1)}, u32[]{:S(2)}, u32[]{:S(2)}) collective-permute-start(bf16[32,1536]{1,0:T(8,128)(2,1)S(1)} %collective-permute-done.13), channel_id=1, source_target_pairs={{192,256},{448,512},{704,768},{193,257},{449,513},{705,769},{194,2... | collective-permute-start | bytes 294920 | tf_op jit(solution)/shard_map/ppermute | solution.py:325
  141.8 30.9 %collective-permute-start.23 = (bf16[48,1536]{1,0:T(8,128)(2,1)S(1)}, bf16[48,1536]{1,0:T(8,128)(2,1)S(1)}, u32[]{:S(2)}, u32[]{:S(2)}) collective-permute-start(bf16[48,1536]{1,0:T(8,128)(2,1)S(1)} %collective-permute-done.22), channel_id=1, source_target_pairs={{960,0},{961,1},{962,2},{963,3},{964,4},{965,5},{966,6},{967,7}} | collective-permute-start | bytes 442376 | tf_op jit(solution)/shard_map/ppermute | solution.py:325
  142.5 17.5 %collective-permute-start.16 = (bf16[32,1536]{1,0:T(8,128)(2,1)}, bf16[32,1536]{1,0:T(8,128)(2,1)S(1)}, u32[]{:S(2)}, u32[]{:S(2)}) collective-permute-start(bf16[32,1536]{1,0:T(8,128)(2,1)} %collective-permute-done.15), channel_id=1, source_target_pairs={{48,256},{304,512},{560,768},{49,257},{305,513},{561,769},{50,258}... | collective-permute-start | bytes 294920 | tf_op jit(solution)/shard_map/ppermute | solution.py:325
  157.8 14.8 %collective-permute-start.18 = (bf16[32,1536]{1,0:T(8,128)(2,1)}, bf16[32,1536]{1,0:T(8,128)(2,1)S(1)}, u32[]{:S(2)}, u32[]{:S(2)}) collective-permute-start(bf16[32,1536]{1,0:T(8,128)(2,1)} %collective-permute-done.17), channel_id=1, source_target_pairs={{8,256},{264,512},{520,768},{9,257},{265,513},{521,769},{10,258},{... | collective-permute-start | bytes 294920 | tf_op jit(solution)/shard_map/ppermute | solution.py:325
  172.7 3.1 %copy-start.2 = (f32[128,128]{1,0:T(8,128)S(1)}, f32[128,128]{1,0:T(8,128)}, u32[]{:S(2)}) copy-start(f32[128,128]{1,0:T(8,128)} %get-tuple-element.18.shares) | copy-start | bytes 196612
